TPU v7x, 128 devices: a whole 4x4x4 slice. The times are simulated.
128 devices in a mesh: group: 16 (over y, x), tensor: 8 (over z, core).
Axes of the slice: x: 4, y: 4, z: 4, core: 2. Of those that a mesh axis runs over, the one named last changes fastest.
Arguments:
- left_table: bfloat16 [1024, 8, 8192], P('group', 'tensor'), may hold values from -6 to 6
- right_table: bfloat16 [1024, 8, 8192], P('group', 'tensor'), may hold values from -6 to 6
- left_owner: int32 [256, 1], P('group'), may hold values from 0 to 15; in each aligned block of 16 rows (0 to 15, 16 to 31, ...) at most 2 rows name the same one
- left_row: int32 [256], P('group'), may hold values from 0 to 63
- right_owner: int32 [256, 1], P('group'), may hold values from 0 to 15; in each aligned block of 16 rows (0 to 15, 16 to 31, ...) at most 2 rows name the same one
- right_row: int32 [256], P('group'), may hold values from 0 to 63
- pair_count: int32 [16], P('group'), may hold values from 1 to 16, 128 in all
- norm_gain: float32 [8192], replicated, may hold values from 0.1 to 1.9
- query_weight: bfloat16 [8192, 4096], P(None, 'tensor'), may hold values from -0.0625 to 0.0625
- key_weight: bfloat16 [8192, 1024], P(None, 'tensor'), may hold values from -0.0625 to 0.0625
- value_weight: bfloat16 [8192, 1024], P(None, 'tensor'), may hold values from -0.0625 to 0.0625
- output_weight: bfloat16 [4096, 8192], P('tensor'), may hold values from -0.09375 to 0.09375
Outputs:
- left_sums: float32 [1024, 8192], P('group', 'tensor')
- right_sums: float32 [1024, 8192], P('group', 'tensor')
Inputs may be any that keep to these rules, and one draw needn't show every extreme that they name: `left_owner`: among the 16 pair slots of one group, at most 2 have the same left owner; some owner is named by exactly 2 of them in some groups. `right_owner`: among the 16 pair slots of one group, at most 2 have the same right owner; some owner is named by exactly 2 of them in some groups. `pair_count`: the counts sum to 128 and one group has all 16 slots live.
All inputs are finite; a program needn't handle non-finite values.
Results may differ from a plain program's by a relative error of at most 0.0035.
Values may be sent and summed in bfloat16 or wider, within the bound.
A program may use at most 128 MiB of HBM per device.

v0:
```python
import jax
import jax.numpy as jnp
from jax import lax
from jax.sharding import PartitionSpec as P

HEAD_DIM = 128


score_scale = 4.0


def slot_plan(owner, groups, capacity):
    count = owner.shape[0]
    order = jnp.arange(count, dtype=jnp.int32)
    same_owner = owner[:, None] == owner[None, :]
    earlier = order[None, :] < order[:, None]
    rank = jnp.sum(jnp.logical_and(same_owner, earlier), axis=1)
    owner_hit = owner[:, None, None] == jnp.arange(groups, dtype=jnp.int32)[None, :, None]
    rank_hit = rank[:, None, None] == jnp.arange(capacity, dtype=jnp.int32)[None, None, :]
    return (rank, jnp.logical_and(owner_hit, rank_hit))


def request_ids(slot_match, row_index):
    return jnp.sum(jnp.where(slot_match, row_index[:, None, None], 0), axis=0)


def owner_sums(row_ids, arrived, rows_here):
    onehot = (row_ids[:, :, None] == jnp.arange(rows_here, dtype=jnp.int32)[None, None, :]).astype(
        jnp.float32
    )
    return jnp.einsum("gcr,gcf->rf", onehot, arrived, precision=lax.Precision.HIGHEST)


def on_device(
    left_table,
    right_table,
    left_owner,
    left_row,
    right_owner,
    right_row,
    pair_count,
    norm_gain,
    query_weight,
    key_weight,
    value_weight,
    output_weight,
):
    groups = lax.axis_size("group")
    tensors = lax.axis_size("tensor")
    pairs_here = left_owner.shape[0]
    capacity = 2 * pairs_here // groups
    rows_here = left_table.shape[0]
    width = left_table.shape[2]
    feature_share = width // tensors
    left_group = left_owner[:, 0]
    right_group = right_owner[:, 0]
    left_rank, left_match = slot_plan(left_group, groups, capacity)
    right_rank, right_match = slot_plan(right_group, groups, capacity)
    left_request = request_ids(left_match, left_row)
    right_request = request_ids(right_match, right_row)
    left_spread = jnp.broadcast_to(left_request[:, None, :], (groups, tensors, capacity)).reshape(
        groups * tensors, capacity
    )
    right_spread = jnp.broadcast_to(right_request[:, None, :], (groups, tensors, capacity)).reshape(
        groups * tensors, capacity
    )
    left_wanted, right_wanted = (
        lax.all_to_all(left_spread, ("group", "tensor"), split_axis=0, concat_axis=0, tiled=True),
        lax.all_to_all(right_spread, ("group", "tensor"), split_axis=0, concat_axis=0, tiled=True),
    )
    left_back, right_back = (
        lax.all_to_all(
            left_table[left_wanted], ("group", "tensor"), split_axis=0, concat_axis=0, tiled=True
        ),
        lax.all_to_all(
            right_table[right_wanted], ("group", "tensor"), split_axis=0, concat_axis=0, tiled=True
        ),
    )
    left_back = left_back.reshape(groups, tensors, capacity, left_table.shape[1], width)
    right_back = right_back.reshape(groups, tensors, capacity, right_table.shape[1], width)
    left_tokens = left_back[left_group, :, left_rank].reshape(
        pairs_here, tensors * left_table.shape[1], width
    )
    right_tokens = right_back[right_group, :, right_rank].reshape(
        pairs_here, tensors * right_table.shape[1], width
    )
    left_owned = left_wanted.reshape(groups, tensors, capacity)[:, 0]
    right_owned = right_wanted.reshape(groups, tensors, capacity)[:, 0]
    inputs = jnp.concatenate([left_tokens, right_tokens], axis=1)
    length = inputs.shape[1]
    flat = inputs.reshape(pairs_here * length, width)
    wide = flat.astype(jnp.float32)
    scale = lax.rsqrt(jnp.mean(wide * wide, axis=-1, keepdims=True) + 1e-05)
    normed = (wide * scale * norm_gain[None, :]).astype(jnp.bfloat16)
    q_raw = jnp.dot(normed, query_weight, preferred_element_type=jnp.float32)
    k_raw = jnp.dot(normed, key_weight, preferred_element_type=jnp.float32)
    values = jnp.dot(normed, value_weight, preferred_element_type=jnp.float32).astype(jnp.bfloat16)
    kv_local = key_weight.shape[1] // HEAD_DIM
    share = query_weight.shape[1] // HEAD_DIM // kv_local
    q_heads = q_raw.reshape(pairs_here * length, kv_local * share, HEAD_DIM)
    k_heads = k_raw.reshape(pairs_here * length, kv_local, HEAD_DIM)
    q_norm = (
        q_heads * lax.rsqrt(jnp.mean(q_heads * q_heads, axis=-1, keepdims=True) + 1e-06)
    ).astype(jnp.bfloat16)
    k_norm = (
        k_heads * lax.rsqrt(jnp.mean(k_heads * k_heads, axis=-1, keepdims=True) + 1e-06)
    ).astype(jnp.bfloat16)
    q_five = q_norm.reshape(pairs_here, length, kv_local, share, HEAD_DIM)
    k_four = k_norm.reshape(pairs_here, length, kv_local, HEAD_DIM)
    v_four = values.reshape(pairs_here, length, kv_local, HEAD_DIM)
    scores = jnp.einsum("pqkgd,pskd->pkgqs", q_five, k_four, preferred_element_type=jnp.float32) * (
        score_scale / HEAD_DIM
    )
    expo = jnp.exp(scores)
    weights = (expo / jnp.sum(expo, axis=-1, keepdims=True)).astype(jnp.bfloat16)
    context = jnp.einsum(
        "pkgqs,pskd->pqkgd", weights, v_four, preferred_element_type=jnp.float32
    ).astype(jnp.bfloat16)
    context = context.reshape(pairs_here * length, kv_local * share * HEAD_DIM)
    attended = jnp.dot(context, output_weight, preferred_element_type=jnp.float32)
    head_term = jnp.mean(attended.reshape(pairs_here, length, width), axis=1)
    head_part = lax.psum_scatter(head_term, "tensor", scatter_dimension=1, tiled=True)
    feature_start = lax.axis_index("tensor") * feature_share
    own_features = lax.dynamic_slice_in_dim(inputs, feature_start, feature_share, 2)
    residual_mean = jnp.mean(own_features.astype(jnp.float32), axis=1)
    live = jnp.arange(pairs_here, dtype=jnp.int32) < pair_count[0]
    pooled = jnp.where(live[:, None], residual_mean + head_part, jnp.zeros_like(head_part))
    left_send = jnp.einsum(
        "pgc,pf->gcf", left_match.astype(jnp.float32), pooled, precision=lax.Precision.HIGHEST
    )
    right_send = jnp.einsum(
        "pgc,pf->gcf", right_match.astype(jnp.float32), pooled, precision=lax.Precision.HIGHEST
    )
    left_got, right_got = (
        lax.all_to_all(left_send, "group", split_axis=0, concat_axis=0, tiled=True),
        lax.all_to_all(right_send, "group", split_axis=0, concat_axis=0, tiled=True),
    )
    left_sums = owner_sums(left_owned, left_got, rows_here)
    right_sums = owner_sums(right_owned, right_got, rows_here)
    return (left_sums, right_sums)


def solution(mesh):
    return jax.shard_map(
        on_device,
        mesh=mesh,
        in_specs=(
            P("group", "tensor", None),
            P("group", "tensor", None),
            P("group", None),
            P("group"),
            P("group", None),
            P("group"),
            P("group"),
            P(),
            P(None, "tensor"),
            P(None, "tensor"),
            P(None, "tensor"),
            P("tensor", None),
        ),
        out_specs=(P("group", "tensor"), P("group", "tensor")),
        check_vma=False,
    )
```

profile of v0, /device:TPU:0, one launch (start us, length us, event | category | flops | bytes accessed | tf_op | source)
XLA Modules:
  0.0 287.2 jit_solution(7219270551501542994)
XLA Ops:
  10.3 11.1 %all-to-all-start.2 = ((s32[128,1,2]{2,1,0:T(1,128)}), s32[128,1,2]{2,1,0:T(1,128)S(1)}, u32[]{:S(2)}, u32[]{:S(2)}) async-start(s32[128,1,2]{2,1,0:T(1,128)} %bitcast.12), calls=%async_computation.2 | async-start | bytes 131072 | tf_op jit(solution)/shard_map/all_to_all | solution.py:69
  23.8 7.1 %all-to-all-done.2 = s32[128,1,2]{2,1,0:T(1,128)S(1)} async-done(((s32[128,1,2]{2,1,0:T(1,128)}), s32[128,1,2]{2,1,0:T(1,128)S(1)}, u32[]{:S(2)}, u32[]{:S(2)}) %all-to-all-start.2) | async-done | bytes 1056 | tf_op jit(solution)/shard_map/all_to_all | solution.py:69
  31.5 4.6 %all-to-all-start = ((s32[128,1,2]{2,1,0:T(1,128)}), s32[128,1,2]{2,1,0:T(1,128)S(1)}, u32[]{:S(2)}, u32[]{:S(2)}) async-start(s32[128,1,2]{2,1,0:T(1,128)} %bitcast.1), calls=%async_computation | async-start | bytes 131072 | tf_op jit(solution)/shard_map/all_to_all | solution.py:68
  36.2 9.3 %all-to-all-done = s32[128,1,2]{2,1,0:T(1,128)S(1)} async-done(((s32[128,1,2]{2,1,0:T(1,128)}), s32[128,1,2]{2,1,0:T(1,128)S(1)}, u32[]{:S(2)}, u32[]{:S(2)}) %all-to-all-start) | async-done | bytes 1056 | tf_op jit(solution)/shard_map/all_to_all | solution.py:68
  45.7 10.3 %gather_fusion.2 = bf16[256,8192]{1,0:T(8,128)(2,1)} fusion(bf16[64,8192]{1,0:T(8,128)(2,1)} %bitcast.92, s32[1024]{0:T(1024)S(1)} %get-tuple-element.8), kind=kCustom, calls=%fused_computation.2 | custom fusion | bytes 8389632 | tf_op jit(solution)/shard_map/gather | solution.py:76
  56.0 7.6 %reshape.380 = bf16[128,2,1,8192]{3,1,0,2:T(2,128)(2,1)} reshape(bf16[256,8192]{1,0:T(8,128)(2,1)} %gather_fusion.2) | data formatting | bytes 8388608 | tf_op jit(solution)/shard_map/gather | solution.py:76
  63.6 6.1 %all-to-all-start.3 = ((bf16[128,2,1,8192]{3,1,2,0:T(2,128)(2,1)}), bf16[128,2,1,8192]{3,1,2,0:T(2,128)(2,1)}, u32[]{:S(2)}, u32[]{:S(2)}) async-start(bf16[128,2,1,8192]{3,1,2,0:T(2,128)(2,1)} %bitcast.95), calls=%async_computation.3 | async-start | bytes 8388608 | tf_op jit(solution)/shard_map/all_to_all | solution.py:75
  69.8 5.2 %gather_fusion = bf16[256,8192]{1,0:T(8,128)(2,1)} fusion(bf16[64,8192]{1,0:T(8,128)(2,1)S(1)} %bitcast.93, s32[1024]{0:T(1024)S(1)} %get-tuple-element.9), kind=kCustom, calls=%fused_computation | custom fusion | bytes 8389632 | tf_op jit(solution)/shard_map/gather | solution.py:73
  74.9 7.6 %reshape.362 = bf16[128,2,1,8192]{3,1,0,2:T(2,128)(2,1)} reshape(bf16[256,8192]{1,0:T(8,128)(2,1)} %gather_fusion) | data formatting | bytes 8388608 | tf_op jit(solution)/shard_map/gather | solution.py:73
  82.6 39.5 %all-to-all-done.3 = bf16[128,2,1,8192]{3,1,2,0:T(2,128)(2,1)} async-done(((bf16[128,2,1,8192]{3,1,2,0:T(2,128)(2,1)}), bf16[128,2,1,8192]{3,1,2,0:T(2,128)(2,1)}, u32[]{:S(2)}, u32[]{:S(2)}) %all-to-all-start.3) | async-done | bytes 4194336 | tf_op jit(solution)/shard_map/all_to_all | solution.py:75
  122.1 5.8 %all-to-all-start.1 = ((bf16[128,2,1,8192]{3,1,2,0:T(2,128)(2,1)}), bf16[128,2,1,8192]{3,1,2,0:T(2,128)(2,1)}, u32[]{:S(2)}, u32[]{:S(2)}) async-start(bf16[128,2,1,8192]{3,1,2,0:T(2,128)(2,1)} %bitcast.94), calls=%async_computation.1 | async-start | bytes 8388608 | tf_op jit(solution)/shard_map/all_to_all | solution.py:72
  128.0 11.4 %copy.61 = bf16[512,8192]{1,0:T(8,128)(2,1)} copy(bf16[512,8192]{0,1:T(8,128)(2,1)} %bitcast.96) | data formatting | bytes 16777216 | tf_op jit(solution)/shard_map/dot_general | solution.py:95
  139.5 6.8 %copy.41 = bf16[16,8,2,8192]{3,1,2,0:T(8,128)(2,1)} copy(bf16[16,8,2,8192]{3,2,1,0:T(2,128)(2,1)} %bitcast.15) | data formatting | bytes 8388608 | tf_op jit(solution)/shard_map/reshape | solution.py:80
  146.2 34.2 %all-to-all-done.1 = bf16[128,2,1,8192]{3,1,2,0:T(2,128)(2,1)} async-done(((bf16[128,2,1,8192]{3,1,2,0:T(2,128)(2,1)}), bf16[128,2,1,8192]{3,1,2,0:T(2,128)(2,1)}, u32[]{:S(2)}, u32[]{:S(2)}) %all-to-all-start.1) | async-done | bytes 4194336 | tf_op jit(solution)/shard_map/all_to_all | solution.py:72
  180.4 6.8 %copy.37 = bf16[16,8,2,8192]{3,1,2,0:T(8,128)(2,1)} copy(bf16[16,8,2,8192]{3,2,1,0:T(2,128)(2,1)} %bitcast.7) | data formatting | bytes 8388608 | tf_op jit(solution)/shard_map/reshape | solution.py:79
  187.2 4.2 %gather_fusion.1 = bf16[16,8,8192]{2,1,0:T(8,128)(2,1)} fusion(bf16[16,8,2,8192]{3,1,2,0:T(8,128)(2,1)} %copy.37, s32[16]{0:T(128)S(1)} %fusion.41), kind=kCustom, calls=%fused_computation.1 | custom fusion | bytes 4194432 | tf_op jit(solution)/shard_map/gather | solution.py:81
  191.4 3.1 %constant_dynamic-update-slice_fusion.1 = bf16[16,16,8192]{2,1,0:T(8,128)(2,1)} fusion(bf16[16,8,8192]{2,1,0:T(8,128)(2,1)} %gather_fusion.1), kind=kLoop, calls=%fused_computation.63 | loop fusion | bytes 4194304
  194.5 4.2 %gather_fusion.3 = bf16[16,8,8192]{2,1,0:T(8,128)(2,1)} fusion(bf16[16,8,2,8192]{3,1,2,0:T(8,128)(2,1)} %copy.41, s32[16]{0:T(128)S(1)} %fusion.40), kind=kCustom, calls=%fused_computation.3 | custom fusion | bytes 4194432 | tf_op jit(solution)/shard_map/gather | solution.py:84
  198.7 3.1 %constant_dynamic-update-slice_fusion = bf16[16,16,8192]{2,1,0:T(8,128)(2,1)} fusion(bf16[16,16,8192]{2,1,0:T(8,128)(2,1)} %constant_dynamic-update-slice_fusion.1, bf16[16,8,8192]{2,1,0:T(8,128)(2,1)} %gather_fusion.3), kind=kLoop, calls=%fused_computation.62 | loop fusion | bytes 4194304 | tf_op jit(solution)/shard_map/concatenate | solution.py:89
  201.8 3.1 %multiply_reduce_fusion = f32[16,16]{1,0:T(8,128)S(1)} fusion(bf16[16,16,8192]{2,1,0:T(8,128)(2,1)} %constant_dynamic-update-slice_fusion), kind=kLoop, calls=%fused_computation.10 | loop fusion | flops 6291200 | bytes 4195328 | tf_op jit(solution)/shard_map/reduce_sum | solution.py:93
  205.0 3.5 %multiply_convert_fusion = bf16[16,16,8192]{2,1,0:T(8,128)(2,1)S(1)} fusion(bf16[16,16,8192]{2,1,0:T(8,128)(2,1)} %constant_dynamic-update-slice_fusion, f32[8192]{0:T(1024)S(1)} %copy-done.4, f32[16,16]{1,0:T(8,128)S(1)} %add_rsqrt_fusion), kind=kLoop, calls=%fused_computation.9 | loop fusion | flops 8388608 | bytes 8422400 | tf_op jit(solution)/shard_map/convert_element_type | solution.py:94
  208.5 1.2 fusion.3
  210.1 1.3 convolution_convert_fusion.1
  211.4 1.4 multiply_reduce_fusion.2
  212.9 2.8 multiply_reduce_fusion.1
  217.3 5.9 %fusion.4 = f32[16,8192]{1,0:T(8,128)S(1)} fusion(bf16[16,16,512]{2,1,0:T(8,128)(2,1)S(1)} %dot_general.43, bf16[512,8192]{1,0:T(8,128)(2,1)} %param.23), kind=kOutput, calls=%fused_computation.11 | convolution fusion | flops 2149449728 | bytes 9175040 | tf_op jit(solution)/shard_map/dot_general | solution.py:120
  224.7 1.2 convert_reduce_fusion
  225.9 25.2 %reduce-scatter.2.cloned.1.call-done = f32[16,1024]{1,0:T(8,128)} async-done(((f32[16,8192]{1,0:T(8,128)}), f32[16,1024]{1,0:T(8,128)}) %reduce-scatter.2.cloned.1.call-update) | async-done | bytes 65552 | tf_op jit(solution)/shard_map/reduce_scatter | solution.py:122
  253.0 6.8 %all-to-all-start.4 = ((f32[16,2,1024]{2,1,0:T(2,128)}), f32[16,2,1024]{2,1,0:T(2,128)S(1)}, u32[]{:S(2)}, u32[]{:S(2)}) async-start(f32[16,2,1024]{2,1,0:T(2,128)} %copy.46), calls=%async_computation.5 | async-start | bytes 262144 | tf_op jit(solution)/shard_map/all_to_all | solution.py:135
  261.7 6.1 %all-to-all-done.4 = f32[16,2,1024]{2,1,0:T(2,128)S(1)} async-done(((f32[16,2,1024]{2,1,0:T(2,128)}), f32[16,2,1024]{2,1,0:T(2,128)S(1)}, u32[]{:S(2)}, u32[]{:S(2)}) %all-to-all-start.4) | async-done | bytes 131104 | tf_op jit(solution)/shard_map/all_to_all | solution.py:135
  267.8 3.5 %all-to-all-start.5 = ((f32[16,2,1024]{2,1,0:T(2,128)}), f32[16,2,1024]{2,1,0:T(2,128)S(1)}, u32[]{:S(2)}, u32[]{:S(2)}) async-start(f32[16,2,1024]{2,1,0:T(2,128)} %copy.49), calls=%async_computation.6 | async-start | bytes 262144 | tf_op jit(solution)/shard_map/all_to_all | solution.py:136
  272.6 6.7 %all-to-all-done.5 = f32[16,2,1024]{2,1,0:T(2,128)S(1)} async-done(((f32[16,2,1024]{2,1,0:T(2,128)}), f32[16,2,1024]{2,1,0:T(2,128)S(1)}, u32[]{:S(2)}, u32[]{:S(2)}) %all-to-all-start.5) | async-done | bytes 131104 | tf_op jit(solution)/shard_map/all_to_all | solution.py:136
  (62 shorter events, 15.4 us)
Async XLA Ops:
  7.2 204.2 %copy-start = (bf16[8192,128]{1,0:T(8,128)(2,1)S(1)}, bf16[8192,128]{1,0:T(8,128)(2,1)}, u32[]{:S(2)}) copy-start(bf16[8192,128]{1,0:T(8,128)(2,1)} %param.21) | copy-start | bytes 6291460
  10.3 20.6 %all-to-all-start.2 = ((s32[128,1,2]{2,1,0:T(1,128)}), s32[128,1,2]{2,1,0:T(1,128)S(1)}, u32[]{:S(2)}, u32[]{:S(2)}) async-start(s32[128,1,2]{2,1,0:T(1,128)} %bitcast.12), calls=%async_computation.2 | async-start | bytes 131072 | tf_op jit(solution)/shard_map/all_to_all | solution.py:69
  31.5 14.0 %all-to-all-start = ((s32[128,1,2]{2,1,0:T(1,128)}), s32[128,1,2]{2,1,0:T(1,128)S(1)}, u32[]{:S(2)}, u32[]{:S(2)}) async-start(s32[128,1,2]{2,1,0:T(1,128)} %bitcast.1), calls=%async_computation | async-start | bytes 131072 | tf_op jit(solution)/shard_map/all_to_all | solution.py:68
  63.6 6.1 %copy-start.1 = (bf16[64,1,8192]{2,0,1:T(8,128)(2,1)S(1)}, bf16[64,1,8192]{2,0,1:T(8,128)(2,1)}, u32[]{:S(2)}) copy-start(bf16[64,1,8192]{2,0,1:T(8,128)(2,1)} %param.12) | copy-start | bytes 3145732
  63.6 58.5 %all-to-all-start.3 = ((bf16[128,2,1,8192]{3,1,2,0:T(2,128)(2,1)}), bf16[128,2,1,8192]{3,1,2,0:T(2,128)(2,1)}, u32[]{:S(2)}, u32[]{:S(2)}) async-start(bf16[128,2,1,8192]{3,1,2,0:T(2,128)(2,1)} %bitcast.95), calls=%async_computation.3 | async-start | bytes 8388608 | tf_op jit(solution)/shard_map/all_to_all | solution.py:75
  122.1 58.3 %all-to-all-start.1 = ((bf16[128,2,1,8192]{3,1,2,0:T(2,128)(2,1)}), bf16[128,2,1,8192]{3,1,2,0:T(2,128)(2,1)}, u32[]{:S(2)}, u32[]{:S(2)}) async-start(bf16[128,2,1,8192]{3,1,2,0:T(2,128)(2,1)} %bitcast.94), calls=%async_computation.1 | async-start | bytes 8388608 | tf_op jit(solution)/shard_map/all_to_all | solution.py:72
  127.9 123.2 %reduce-scatter.2.cloned.1.call-start = ((), (), s32[]{:S(2)}) async-start(), calls=%async_computation.7 | async-start | bytes 589824 | tf_op jit(solution)/shard_map/reduce_scatter | solution.py:122
  128.0 11.4 %copy-start.5 = (s32[16,1]{0,1:T(1,128)S(1)}, s32[16,1]{0,1:T(1,128)}, u32[]{:S(2)}) copy-start(s32[16,1]{0,1:T(1,128)} %param.14) | copy-start | bytes 196
  128.0 11.4 %copy-start.6 = (s32[16,1]{0,1:T(1,128)S(1)}, s32[16,1]{0,1:T(1,128)}, u32[]{:S(2)}) copy-start(s32[16,1]{0,1:T(1,128)} %param.16) | copy-start | bytes 196
  198.7 6.3 %copy-start.4 = (f32[8192]{0:T(1024)S(1)}, f32[8192]{0:T(1024)}, u32[]{:S(2)}) copy-start(f32[8192]{0:T(1024)} %param.19) | copy-start | bytes 98308
  205.0 3.5 %copy-start.2 = (bf16[16,16,8192]{2,1,0:T(8,128)(2,1)S(1)}, bf16[16,16,8192]{2,1,0:T(8,128)(2,1)}, u32[]{:S(2)}) copy-start(bf16[16,16,8192]{2,1,0:T(8,128)(2,1)} %constant_dynamic-update-slice_fusion) | copy-start | bytes 12582916
  208.5 1.6 copy-start.3
  208.5 4.3 %slice-start = ((s8[8388608]{0:T(1024)(128)(4,1)}), s8[4194304]{0:T(1024)(128)(4,1)S(1)}, s32[]{:S(2)}) async-start(s8[8388608]{0:T(1024)(128)(4,1)} %bitcast.97), calls=%async_computation.8 | async-start | bytes 8388608
  210.1 2.8 slice-start.1
  253.0 14.8 %all-to-all-start.4 = ((f32[16,2,1024]{2,1,0:T(2,128)}), f32[16,2,1024]{2,1,0:T(2,128)S(1)}, u32[]{:S(2)}, u32[]{:S(2)}) async-start(f32[16,2,1024]{2,1,0:T(2,128)} %copy.46), calls=%async_computation.5 | async-start | bytes 262144 | tf_op jit(solution)/shard_map/all_to_all | solution.py:135
  267.8 11.5 %all-to-all-start.5 = ((f32[16,2,1024]{2,1,0:T(2,128)}), f32[16,2,1024]{2,1,0:T(2,128)S(1)}, u32[]{:S(2)}, u32[]{:S(2)}) async-start(f32[16,2,1024]{2,1,0:T(2,128)} %copy.49), calls=%async_computation.6 | async-start | bytes 262144 | tf_op jit(solution)/shard_map/all_to_all | solution.py:136
Sparse Core Ops, SparseCore 0:
  224.2 26.9 reduce-scatter.1
where the time goes:
time: 289 us; the launch traced here: 287 us
  waiting for transfers between devices  128 us (44%)
  local copies, waits for them, and re-layouts  74.4 us (26%)
  starting transfers between devices  38.1 us (13%)
  matrix products  16.8 us (6%)
  between operations  15 us (5%)
  other arithmetic  14.8 us (5%)
    all_to_all x1, waiting for transfers between devices, on_device(): lax.all_to_all(right_table[right_wanted], ('group', 'tensor'), split_axis...  39.5 us
    all_to_all x1, waiting for transfers between devices, on_device(): lax.all_to_all(left_table[left_wanted], ('group', 'tensor'), split_axis=0...  34.2 us
    reduce_scatter x1, waiting for transfers between devices, on_device(): lax.psum_scatter(head_term, 'tensor', scatter_dimension=1, tiled=True)  25.2 us
    gather x2, local copies, waits for them, and re-layouts, on_device(): right_table[right_wanted]  17.9 us
    gather x2, local copies, waits for them, and re-layouts, on_device(): left_table[left_wanted]  12.8 us
    dot_general x1, local copies, waits for them, and re-layouts, on_device(): q_raw = jnp.dot(normed, query_weight, preferred_element_type=jnp.float32)  11.4 us
    all_to_all x1, starting transfers between devices, on_device(): lax.all_to_all(right_spread, ('group', 'tensor'), split_axis=0, concat_ax...  11.1 us
    all_to_all x1, waiting for transfers between devices, on_device(): lax.all_to_all(left_spread, ('group', 'tensor'), split_axis=0, concat_axi...  9.28 us
  transfers between devices with their start and end apart: 7, of which 7 were waited for; matrix products, arithmetic and copies ran while one was open for 13% of the time, Pallas kernels for 0%

commit v1 on v0

v1 whole, which is shorter than its diff:
```python
import functools

import jax
import jax.numpy as jnp
from jax import lax
from jax.experimental import pallas as pl
from jax.experimental.pallas import tpu as pltpu
from jax.sharding import PartitionSpec as P

HEAD_DIM = 128
SCORE_SCALE = 4.0
MESH = pl.DeviceIdType.MESH
GROUPS = 16
SIDE = 4
TENSORS = 8
PAIRS = 16
SLOTS = GROUPS * 8
ROWS = 64
F32 = jnp.float32
BF16 = jnp.bfloat16


def iota(shape, axis):
    return lax.broadcasted_iota(jnp.int32, shape, axis)


def group_shift(g, k, sign):
    y, x = g // SIDE, g % SIDE
    ky, kx = k // SIDE, k % SIDE
    return ((y + sign * ky + SIDE) % SIDE) * SIDE + (x + sign * kx + SIDE) % SIDE


def pieces(value):
    high = value.astype(BF16)
    rest = value - high.astype(F32)
    middle = rest.astype(BF16)
    low = (rest - middle.astype(F32)).astype(BF16)
    return high, middle, low


def to_column(row):
    eye = iota((PAIRS, PAIRS), 0) == iota((PAIRS, PAIRS), 1)
    return jnp.sum(jnp.where(eye, row, 0.0), axis=1, keepdims=True)


def slot_keys(owner_row, me):
    owner_col = to_column(owner_row)
    first = iota((PAIRS, PAIRS), 0)
    second = iota((PAIRS, PAIRS), 1)
    same = owner_col == owner_row
    rank_row = jnp.sum(jnp.where(same & (first < second), 1.0, 0.0), axis=0, keepdims=True)
    rank_col = jnp.sum(jnp.where(same & (second < first), 1.0, 0.0), axis=1, keepdims=True)
    want_row = owner_row * 2.0 + rank_row

    def place(owner, rank):
        whole = owner.astype(jnp.int32)
        y, x = me // SIDE, me % SIDE
        ky = (y - whole // SIDE + SIDE) % SIDE
        kx = (x - whole % SIDE + SIDE) % SIDE
        return ((ky * SIDE + kx) * 2).astype(F32) + rank

    return want_row, place(owner_row, rank_row), place(owner_col, rank_col)


def requests(want_row, row_row, me):
    sub = iota((SLOTS, PAIRS), 0)
    k = sub // 8
    y, x = me // SIDE, me % SIDE
    owner = ((y - k // SIDE + SIDE) % SIDE) * SIDE + (x - k % SIDE + SIDE) % SIDE
    want = (owner * 2 + sub % 2).astype(F32)
    found = jnp.sum(jnp.where(want_row == want, row_row + 1.0, 0.0), axis=1, keepdims=True) - 1.0
    return jnp.broadcast_to(found, (SLOTS, 128))


def pick_matrix(wanted):
    both = jnp.concatenate([wanted, wanted], axis=1)
    lane = iota((SLOTS, 4 * ROWS), 1)
    quarter = (iota((SLOTS, 4 * ROWS), 0) % 8) // 2
    hit = (both == (lane % ROWS).astype(F32)) & (lane // ROWS == quarter)
    return jnp.where(hit, 1.0, 0.0).astype(BF16)


def pack_matrix(place_col):
    tall = jnp.concatenate([place_col] * 4, axis=0)
    lane = iota((4 * PAIRS, SLOTS), 1)
    quarter = iota((4 * PAIRS, SLOTS), 0) // PAIRS
    key = ((lane // 8) * 2 + lane % 2).astype(F32)
    hit = (tall == key) & ((lane % 8) // 2 == quarter)
    return jnp.where(hit, 1.0, 0.0).astype(BF16)


def spread_matrix(place_row):
    wide = jnp.concatenate([place_row] * 4, axis=1)
    sub = iota((SLOTS, 4 * PAIRS), 0)
    quarter = iota((SLOTS, 4 * PAIRS), 1) // PAIRS
    key = ((sub // 8) * 2 + sub % 2).astype(F32)
    hit = (wide == key) & ((sub % 8) // 2 == quarter)
    return jnp.where(hit, 1.0, 0.0).astype(BF16)


def dot(a, b):
    return jnp.dot(a, b, preferred_element_type=F32)


def kernel(
    lo_ref, lr_ref, ro_ref, rr_ref, count_ref, gain_ref,
    lt_ref, rt_ref, wq_ref, wk_ref, wv_ref, wo_ref,
    lout_ref, rout_ref,
    table, qkv_w, out_w, outbox, inbox, picked, arrived, tokens, flat, resid,
    acc, part, parts_in, fin_out, fin_in,
    load_sem, idx_s, idx_r, row_s, row_r, ag_s, ag_r, rs_s, rs_r, fin_s, fin_r,
):
    g = lax.axis_index("group")
    t = lax.axis_index("tensor")
    z, c = t // 2, t % 2
    width = out_w.shape[1]
    quarter = width // 4
    share = width // TENSORS

    loads = []

    def load(src, dst):
        copy = pltpu.make_async_copy(src, dst, load_sem.at[len(loads)])
        copy.start()
        loads.append(copy)

    for side, ref in enumerate((lt_ref, rt_ref)):
        for q in range(4):
            load(ref.at[:, pl.ds(q * quarter, quarter)], table.at[side, pl.ds(q * ROWS, ROWS), :])

    barrier = pltpu.get_barrier_semaphore()
    for k in range(1, GROUPS):
        pl.semaphore_signal(
            barrier, inc=1, device_id=(group_shift(g, k, 1), t), device_id_type=MESH
        )
    for j in range(1, TENSORS):
        pl.semaphore_signal(
            barrier, inc=1, device_id=(g, (t + j) % TENSORS), device_id_type=MESH
        )

    q_cols = wq_ref.shape[1]
    kv_cols = wk_ref.shape[1]
    load(wq_ref, qkv_w.at[:, pl.ds(0, q_cols)])
    load(wk_ref, qkv_w.at[:, pl.ds(q_cols, kv_cols)])
    load(wv_ref, qkv_w.at[:, pl.ds(q_cols + kv_cols, kv_cols)])
    load(wo_ref, out_w)

    owners = (lo_ref[...].astype(F32), ro_ref[...].astype(F32))
    rows = (lr_ref[...].astype(F32), rr_ref[...].astype(F32))
    keys = [slot_keys(owners[side], g) for side in range(2)]
    for side in range(2):
        asked = requests(keys[side][0], rows[side], g)
        outbox[:, :, pl.ds(side * 128, 128)] = asked.reshape(GROUPS, 8, 128)

    pl.semaphore_wait(barrier, GROUPS - 1 + TENSORS - 1)

    idx = []
    for k in range(1, GROUPS):
        copy = pltpu.make_async_remote_copy(
            src_ref=outbox.at[k], dst_ref=inbox.at[k],
            send_sem=idx_s.at[k], recv_sem=idx_r.at[k],
            device_id=(group_shift(g, k, -1), t), device_id_type=MESH,
        )
        copy.start()
        idx.append(copy)
    inbox[0] = outbox[0]
    for copy in loads[:8]:
        copy.wait()
    for copy in idx:
        copy.wait_recv()

    chunk = 512
    picks = []
    row_copies = [[], []]
    for side in range(2):
        wanted = inbox[:, :, pl.ds(side * 128, 128)].reshape(SLOTS, 128)
        pick = pick_matrix(wanted)
        picks.append(pick)
        for n in range(quarter // chunk):
            cols = pl.ds(n * chunk, chunk)
            picked[side, :, :, cols] = (
                dot(pick, table[side, :, cols]).astype(BF16).reshape(GROUPS, 8, chunk)
            )
        for k in range(1, GROUPS):
            copy = pltpu.make_async_remote_copy(
                src_ref=picked.at[side, k], dst_ref=arrived.at[side, k],
                send_sem=row_s.at[side, k], recv_sem=row_r.at[side, k],
                device_id=(group_shift(g, k, 1), t), device_id_type=MESH,
            )
            copy.start()
            row_copies[side].append(copy)
        arrived[side, 0] = picked[side, 0]

    up = ((z + 1) % SIDE) * 2 + c
    down = ((z + SIDE - 1) % SIDE) * 2 + c
    far = ((z + 2) % SIDE) * 2 + c
    twin = z * 2 + 1 - c

    def send(side, number, block, half, target):
        place = tokens.at[side, block]
        if half is not None:
            place = place.at[pl.ds(half * 8, 8)]
        copy = pltpu.make_async_remote_copy(
            src_ref=place, dst_ref=place,
            send_sem=ag_s.at[side, number], recv_sem=ag_r.at[side, number],
            device_id=(g, target), device_id_type=MESH,
        )
        copy.start()
        return copy

    gathers = [{}, {}]
    for side in range(2):
        for copy in row_copies[side]:
            copy.wait_recv()
        pack = pack_matrix(keys[side][2])
        squares = jnp.zeros((PAIRS, 1), F32)
        for n in range(quarter // chunk):
            cols = pl.ds(n * chunk, chunk)
            got = dot(pack, arrived[side, :, :, cols].reshape(SLOTS, chunk))
            for q in range(4):
                one = got[q * PAIRS : (q + 1) * PAIRS]
                flat[:, pl.ds(q * quarter + n * chunk, chunk)] = one
                squares = squares + jnp.sum(one * one, axis=1, keepdims=True)
        scale = lax.rsqrt(squares / width + 1e-05)
        for n in range(width // chunk):
            cols = pl.ds(n * chunk, chunk)
            one = flat[:, cols]
            tokens[side, t, :, cols] = (one * scale * gain_ref[:, cols]).astype(BF16)
            if side == 0:
                resid[:, cols] = one
            else:
                resid[:, cols] = (resid[:, cols] + one) * (1.0 / 16.0)
        for number, target in ((0, up), (1, down), (2, twin)):
            gathers[side][number] = send(side, number, t, None, target)

    def forward_near(side):
        gathers[side][0].wait_recv()
        gathers[side][3] = send(side, 3, down, 0, up)
        gathers[side][4] = send(side, 4, down, None, twin)
        gathers[side][1].wait_recv()
        gathers[side][5] = send(side, 5, up, 1, down)
        gathers[side][6] = send(side, 6, up, None, twin)

    def forward_far(side):
        gathers[side][3].wait_recv()
        gathers[side][5].wait_recv()
        gathers[side][7] = send(side, 7, far, None, twin)

    def project(side):
        for number in (2, 4, 6, 7):
            gathers[side][number].wait_recv()
        depth = 512
        acc[side] = jnp.zeros_like(acc[side])

        @pl.loop(0, width // depth)
        def _(i):
            cols = pl.ds(pl.multiple_of(i * depth, depth), depth)
            a = tokens[side, :, :, cols].reshape(TENSORS * PAIRS, depth)
            acc[side] += dot(a, qkv_w[cols, :])

    forward_near(0)
    forward_far(0)
    forward_near(1)
    for copy in loads[8:11]:
        copy.wait()
    project(0)
    forward_far(1)
    project(1)

    count = 2 * TENSORS * PAIRS
    full = acc[...].reshape(count, q_cols + 2 * kv_cols)
    key = full[:, q_cols : q_cols + HEAD_DIM]
    value = full[:, q_cols + kv_cols : q_cols + kv_cols + HEAD_DIM].astype(BF16)

    def unit(rows_):
        return (
            rows_ * lax.rsqrt(jnp.mean(rows_ * rows_, axis=-1, keepdims=True) + 1e-06)
        ).astype(BF16)

    key = unit(key)
    mask = (iota((count, count), 0) % PAIRS) == (iota((count, count), 1) % PAIRS)
    pool = jnp.where(
        iota((PAIRS, count), 0) == iota((PAIRS, count), 1) % PAIRS, 1.0, 0.0
    ).astype(BF16)
    pooled = []
    for head in range(q_cols // HEAD_DIM):
        query = unit(full[:, head * HEAD_DIM : (head + 1) * HEAD_DIM])
        scores = lax.dot_general(
            query, key, (((1,), (1,)), ((), ())), preferred_element_type=F32
        ) * (SCORE_SCALE / HEAD_DIM)
        expo = jnp.where(mask, jnp.exp(scores), 0.0)
        weights = (expo / jnp.sum(expo, axis=-1, keepdims=True)).astype(BF16)
        context = dot(weights, value).astype(BF16)
        pooled.append(dot(pool, context) * (1.0 / 16.0))
    pooled = jnp.concatenate(pooled, axis=1)
    high = pooled.astype(BF16)
    low = (pooled - high.astype(F32)).astype(BF16)
    both = jnp.concatenate([high, low], axis=0)

    loads[11].wait()
    sums = []
    for j in (4, 5, 2, 3, 6, 7, 1, 0):
        target = ((z + j // 2) % SIDE) * 2 + (c + j % 2) % 2
        cols = pl.ds(pl.multiple_of(target * share, share), share)
        got = dot(both, out_w[:, cols])
        part[j] = got[:PAIRS] + got[PAIRS:] + resid[:, cols]
        if j > 0:
            copy = pltpu.make_async_remote_copy(
                src_ref=part.at[j], dst_ref=parts_in.at[j],
                send_sem=rs_s.at[j], recv_sem=rs_r.at[j],
                device_id=(g, target), device_id_type=MESH,
            )
            copy.start()
            sums.append(copy)
    for copy in sums:
        copy.wait_recv()
    total = part[0]
    for j in range(1, TENSORS):
        total = total + parts_in[j]
    live = iota((PAIRS, share), 0) < count_ref[...]
    total = jnp.where(live, total, 0.0)

    piece = share // 4
    stacked = jnp.concatenate([total[:, q * piece : (q + 1) * piece] for q in range(4)], axis=0)
    parts3 = pieces(stacked)
    for side in range(2):
        spread = spread_matrix(keys[side][1])
        got = dot(spread, parts3[0]) + dot(spread, parts3[1]) + dot(spread, parts3[2])
        fin_out[:, :, pl.ds(side * piece, piece)] = got.reshape(GROUPS, 8, piece)
    finals = []
    for k in range(1, GROUPS):
        copy = pltpu.make_async_remote_copy(
            src_ref=fin_out.at[k], dst_ref=fin_in.at[k],
            send_sem=fin_s.at[k], recv_sem=fin_r.at[k],
            device_id=(group_shift(g, k, -1), t), device_id_type=MESH,
        )
        copy.start()
        finals.append(copy)
    fin_in[0] = fin_out[0]
    for copy in finals:
        copy.wait_recv()
    for side, out in enumerate((lout_ref, rout_ref)):
        came = pieces(fin_in[:, :, pl.ds(side * piece, piece)].reshape(SLOTS, piece))
        got = jnp.zeros((4 * ROWS, piece), F32)
        for one in came:
            got = got + lax.dot_general(
                picks[side], one, (((0,), (0,)), ((), ())), preferred_element_type=F32
            )
        for q in range(4):
            out[:, pl.ds(q * piece, piece)] = got[q * ROWS : (q + 1) * ROWS]

    for copy in idx + row_copies[0] + row_copies[1] + sums + finals:
        copy.wait_send()
    for side in range(2):
        for copy in gathers[side].values():
            copy.wait_send()


def on_device(
    left_table, right_table, left_owner, left_row, right_owner, right_row, pair_count,
    norm_gain, query_weight, key_weight, value_weight, output_weight,
):
    width = left_table.shape[2]
    quarter = width // 4
    share = width // TENSORS
    qkv = query_weight.shape[1] + 2 * key_weight.shape[1]
    vmem = pl.BlockSpec(memory_space=pltpu.VMEM)
    hbm = pl.BlockSpec(memory_space=pl.ANY)
    dma = pltpu.SemaphoreType.DMA
    out = jax.ShapeDtypeStruct((ROWS, share), F32)
    return pl.pallas_call(
        kernel,
        out_shape=(out, out),
        in_specs=[vmem] * 6 + [hbm] * 6,
        out_specs=(vmem, vmem),
        scratch_shapes=[
            pltpu.VMEM((2, 4 * ROWS, quarter), BF16),
            pltpu.VMEM((width, qkv), BF16),
            pltpu.VMEM(output_weight.shape, BF16),
            pltpu.VMEM((GROUPS, 8, 256), F32),
            pltpu.VMEM((GROUPS, 8, 256), F32),
            pltpu.VMEM((2, GROUPS, 8, quarter), BF16),
            pltpu.VMEM((2, GROUPS, 8, quarter), BF16),
            pltpu.VMEM((2, TENSORS, PAIRS, width), BF16),
            pltpu.VMEM((PAIRS, width), F32),
            pltpu.VMEM((PAIRS, width), F32),
            pltpu.VMEM((2, TENSORS * PAIRS, qkv), F32),
            pltpu.VMEM((TENSORS, PAIRS, share), F32),
            pltpu.VMEM((TENSORS, PAIRS, share), F32),
            pltpu.VMEM((GROUPS, 8, share // 2), F32),
            pltpu.VMEM((GROUPS, 8, share // 2), F32),
            dma((12,)),
            dma((GROUPS,)), dma((GROUPS,)),
            dma((2, GROUPS)), dma((2, GROUPS)),
            dma((2, 8)), dma((2, 8)),
            dma((TENSORS,)), dma((TENSORS,)),
            dma((GROUPS,)), dma((GROUPS,)),
        ],
        compiler_params=pltpu.CompilerParams(
            collective_id=0, has_side_effects=True, vmem_limit_bytes=56 * 1024 * 1024
        ),
    )(
        left_owner.reshape(1, PAIRS), left_row.reshape(1, PAIRS),
        right_owner.reshape(1, PAIRS), right_row.reshape(1, PAIRS),
        pair_count.reshape(1, 1), norm_gain.reshape(1, width),
        left_table.reshape(ROWS, width), right_table.reshape(ROWS, width),
        query_weight, key_weight, value_weight, output_weight,
    )


def solution(mesh):
    return jax.shard_map(
        on_device,
        mesh=mesh,
        in_specs=(
            P("group", "tensor", None), P("group", "tensor", None),
            P("group", None), P("group"), P("group", None), P("group"), P("group"), P(),
            P(None, "tensor"), P(None, "tensor"), P(None, "tensor"), P("tensor", None),
        ),
        out_specs=(P("group", "tensor"), P("group", "tensor")),
        check_vma=False,
    )
```

time: 289 us -> 74.6 us (0.26)
  waiting for transfers between devices: 128 us -> 0 us
  local copies, waits for them, and re-layouts: 74.4 us -> 3.34 us
  Pallas kernels: 0 us -> 69.5 us
  starting transfers between devices: 38.1 us -> 0 us
  matrix products: 16.8 us -> 0 us
  other arithmetic: 14.8 us -> 0 us
  between operations: 15 us -> 1.29 us
    all_to_all x6 -> x0, waiting for transfers between devices: 103 us -> none  [the longest x1 39.5 us: on_device(): lax.all_to_all(right_table[right_wanted], ('group', 'tensor'), split_axis...]
    pallas_call x0 -> x1, Pallas kernels: none -> 69.5 us  [on_device(): pl.pallas_call(kernel, out_shape=(out, out), in_specs=[vmem] * 6 + [hbm]...]
    gather x6 -> x0, local copies, waits for them, and re-layouts: 39.2 us -> none  [the longest x2 17.9 us: on_device(): right_table[right_wanted]]
    all_to_all x6 -> x0, starting transfers between devices: 38 us -> none  [the longest x1 11.1 us: on_device(): lax.all_to_all(right_spread, ('group', 'tensor'), split_axis=0, concat_ax...]
    reduce_scatter x1 -> x0, waiting for transfers between devices: 25.2 us -> none  [on_device(): lax.psum_scatter(head_term, 'tensor', scatter_dimension=1, tiled=True)]
    dot_general x10 -> x0, matrix products: 16.8 us -> none  [the longest x1 5.88 us: on_device(): jnp.dot(context, output_weight, preferred_element_type=jnp.float32)]
    reshape x2 -> x0, local copies, waits for them, and re-layouts: 13.5 us -> none  [the longest x1 6.78 us: on_device(): right_back.reshape(groups, tensors, capacity, right_table.shape[1], width)]
    dot_general x4 -> x0, local copies, waits for them, and re-layouts: 13 us -> none  [the longest x1 11.4 us: on_device(): q_raw = jnp.dot(normed, query_weight, preferred_element_type=jnp.float32)]
  transfers between devices with their start and end apart: 7 -> 0, of which waited for: 7 -> 0; matrix products, arithmetic and copies ran while one was open for 13% -> 0% of each run, Pallas kernels for 0% -> 0%
where the time goes in v1:
time: 74.6 us; the launch traced here: 74.1 us
  Pallas kernels  69.5 us (93%)
  local copies, waits for them, and re-layouts  3.34 us (4%)
  between operations  1.29 us (2%)
    pallas_call x1, Pallas kernels, on_device(): pl.pallas_call(kernel, out_shape=(out, out), in_specs=[vmem] * 6 + [hbm]...  69.5 us
    unnamed x2, local copies, waits for them, and re-layouts  3.34 us

profile of v1, /device:TPU:0, one launch (start us, length us, event | category | flops | bytes accessed | tf_op | source)
XLA Modules:
  0.0 74.1 jit_solution(16355012625818136764)
XLA Ops:
  1.3 69.5 %shard_map.131 = (f32[64,1024]{1,0:T(8,128)}, f32[64,1024]{1,0:T(8,128)}) custom-call(s32[1,16]{1,0:T(1,128)} %bitcast.12, s32[1,16]{1,0:T(1,128)} %bitcast.13, s32[1,16]{1,0:T(1,128)} %bitcast.14, s32[1,16]{1,0:T(1,128)} %bitcast.15, s32[1,1]{1,0:T(1,128)} %bitcast.8.count_ref, f32[1,8192]{1,0:T(1,128)} %bitcast.11, bf16[64,8192]{1,0:T(8,128)(2,1)} %bitcast.9, ...), custom_call_target="tpu_custom_call" | custom-call | tf_op jit(solution)/shard_map/pallas_call | solution.py:371
  70.8 1.7 %copy.17 = f32[64,1024]{1,0:T(8,128)} copy(f32[64,1024]{1,0:T(8,128)} %get-tuple-element.4) | data formatting | bytes 524288
  72.5 1.7 %copy.18 = f32[64,1024]{1,0:T(8,128)} copy(f32[64,1024]{1,0:T(8,128)} %get-tuple-element.5) | data formatting | bytes 524288

commit v2 on v1

v2 whole, which is shorter than its diff:
```python
import jax
import jax.numpy as jnp
from jax import lax
from jax.experimental import pallas as pl
from jax.experimental.pallas import tpu as pltpu
from jax.sharding import PartitionSpec as P

HEAD_DIM = 128
SCORE_SCALE = 4.0
MESH = pl.DeviceIdType.MESH
GROUPS = 16
SIDE = 4
TENSORS = 8
PAIRS = 16
SLOTS = GROUPS * 8
ROWS = 64
CHUNKS = 4
F32 = jnp.float32
BF16 = jnp.bfloat16


def iota(shape, axis):
    return lax.broadcasted_iota(jnp.int32, shape, axis)


def group_shift(g, k, sign):
    y, x = g // SIDE, g % SIDE
    ky, kx = k // SIDE, k % SIDE
    return ((y + sign * ky + SIDE) % SIDE) * SIDE + (x + sign * kx + SIDE) % SIDE


def pieces(value):
    high = value.astype(BF16)
    rest = value - high.astype(F32)
    middle = rest.astype(BF16)
    low = (rest - middle.astype(F32)).astype(BF16)
    return high, middle, low


def to_column(row):
    eye = iota((PAIRS, PAIRS), 0) == iota((PAIRS, PAIRS), 1)
    return jnp.sum(jnp.where(eye, row, 0.0), axis=1, keepdims=True)


def slot_keys(owner_row, me):
    owner_col = to_column(owner_row)
    first = iota((PAIRS, PAIRS), 0)
    second = iota((PAIRS, PAIRS), 1)
    same = owner_col == owner_row
    rank_row = jnp.sum(jnp.where(same & (first < second), 1.0, 0.0), axis=0, keepdims=True)
    rank_col = jnp.sum(jnp.where(same & (second < first), 1.0, 0.0), axis=1, keepdims=True)
    want_row = owner_row * 2.0 + rank_row

    def place(owner, rank):
        whole = owner.astype(jnp.int32)
        y, x = me // SIDE, me % SIDE
        ky = (y - whole // SIDE + SIDE) % SIDE
        kx = (x - whole % SIDE + SIDE) % SIDE
        return ((ky * SIDE + kx) * 2).astype(F32) + rank

    return want_row, place(owner_row, rank_row), place(owner_col, rank_col)


def slot_parts(shape, axis):
    at = iota(shape, axis)
    return at // 8, (at % 8) // 4, (at % 4) // 2, at % 2


def requests(want_rows, row_rows, me):
    k, _, side, rank = slot_parts((SLOTS, PAIRS), 0)
    y, x = me // SIDE, me % SIDE
    owner = ((y - k // SIDE + SIDE) % SIDE) * SIDE + (x - k % SIDE + SIDE) % SIDE
    want = (owner * 2 + rank).astype(F32)
    left = side == 0
    hit = jnp.where(left, want_rows[0], want_rows[1]) == want
    found = jnp.where(hit, jnp.where(left, row_rows[0], row_rows[1]) + 1.0, 0.0)
    return jnp.broadcast_to(jnp.sum(found, axis=1, keepdims=True) - 1.0, (SLOTS, 128))


def pick_matrix(wanted):
    shape = (SLOTS, 4 * ROWS)
    _, half, side, _ = slot_parts(shape, 0)
    lane = iota(shape, 1)
    both = jnp.concatenate([wanted, wanted], axis=1)
    hit = (both == (lane % ROWS).astype(F32)) & (lane // ROWS == half * 2 + side)
    return jnp.where(hit, 1.0, 0.0).astype(BF16)


def pack_matrix(place_cols):
    shape = (4 * PAIRS, SLOTS)
    tall = jnp.concatenate(list(place_cols) * 2, axis=0)
    k, half, side, rank = slot_parts(shape, 1)
    hit = (tall == (k * 2 + rank).astype(F32)) & (iota(shape, 0) // PAIRS == half * 2 + side)
    return jnp.where(hit, 1.0, 0.0).astype(BF16)


def spread_matrix(place_rows):
    shape = (SLOTS, 2 * PAIRS)
    k, half, side, rank = slot_parts(shape, 0)
    wide = [jnp.concatenate([row, row], axis=1) for row in place_rows]
    key = (k * 2 + rank).astype(F32)
    hit = (jnp.where(side == 0, wide[0], wide[1]) == key) & (iota(shape, 1) // PAIRS == half)
    return jnp.where(hit, 1.0, 0.0).astype(BF16)


def dot(a, b):
    return jnp.dot(a, b, preferred_element_type=F32)


def kernel(
    lo_ref, lr_ref, ro_ref, rr_ref, count_ref, gain_ref,
    lt_ref, rt_ref, wq_ref, wk_ref, wv_ref, wo_ref,
    inbox, fin_in,
    table, qkv_w, out_w, outbox, picked, arrived, tokens, scales, resid,
    acc, part, parts_in, fin_out,
    load_sem, idx_s, idx_r, row_s, row_r, ag_s, ag_r, sc_s, sc_r, rs_s, rs_r, fin_s, fin_r,
):
    g = lax.axis_index("group")
    t = lax.axis_index("tensor")
    z, c = t // 2, t % 2
    width = out_w.shape[1]
    half = width // 2
    piece = half // CHUNKS
    share = width // TENSORS

    loads = []

    def load(src, dst):
        copy = pltpu.make_async_copy(src, dst, load_sem.at[len(loads)])
        copy.start()
        loads.append(copy)

    for h in range(2):
        for side, ref in enumerate((lt_ref, rt_ref)):
            load(
                ref.at[:, pl.ds(h * half, half)],
                table.at[pl.ds((h * 2 + side) * ROWS, ROWS), :],
            )

    barrier = pltpu.get_barrier_semaphore()
    for k in range(1, GROUPS):
        pl.semaphore_signal(
            barrier, inc=1, device_id=(group_shift(g, k, 1), t), device_id_type=MESH
        )
    for j in range(1, TENSORS):
        pl.semaphore_signal(
            barrier, inc=1, device_id=(g, (t + j) % TENSORS), device_id_type=MESH
        )

    q_cols = wq_ref.shape[1]
    kv_cols = wk_ref.shape[1]
    load(wq_ref, qkv_w.at[:, pl.ds(0, q_cols)])
    load(wk_ref, qkv_w.at[:, pl.ds(q_cols, kv_cols)])
    load(wv_ref, qkv_w.at[:, pl.ds(q_cols + kv_cols, kv_cols)])
    load(wo_ref, out_w)

    rows = (lr_ref[...].astype(F32), rr_ref[...].astype(F32))
    keys = [slot_keys(ref[...].astype(F32), g) for ref in (lo_ref, ro_ref)]
    asked = requests([key[0] for key in keys], rows, g)
    outbox[...] = asked.reshape(GROUPS, 8, 128)
    pack = pack_matrix([key[2] for key in keys])
    spread = spread_matrix([key[1] for key in keys])

    pl.semaphore_wait(barrier, GROUPS - 1 + TENSORS - 1)

    idx = []
    for k in range(1, GROUPS):
        copy = pltpu.make_async_remote_copy(
            src_ref=outbox.at[k], dst_ref=inbox.at[k],
            send_sem=idx_s.at[k], recv_sem=idx_r.at[k],
            device_id=(group_shift(g, k, -1), t), device_id_type=MESH,
        )
        copy.start()
        idx.append(copy)
    inbox[0] = outbox[0]
    for copy in loads[:4]:
        copy.wait()
    for copy in idx:
        copy.wait_recv()

    pick = pick_matrix(inbox[...].reshape(SLOTS, 128))
    row_copies = []
    for n in range(CHUNKS):
        rows_n = dot(pick, table[:, pl.ds(n * piece, piece)])
        picked[n] = rows_n.astype(BF16).reshape(GROUPS, 8, piece)
        copies = []
        for k in range(1, GROUPS):
            copy = pltpu.make_async_remote_copy(
                src_ref=picked.at[n, k], dst_ref=arrived.at[n, k],
                send_sem=row_s.at[n, k], recv_sem=row_r.at[n, k],
                device_id=(group_shift(g, k, 1), t), device_id_type=MESH,
            )
            copy.start()
            copies.append(copy)
        arrived[n, 0] = picked[n, 0]
        row_copies.append(copies)

    up = ((z + 1) % SIDE) * 2 + c
    down = ((z + SIDE - 1) % SIDE) * 2 + c
    far = ((z + 2) % SIDE) * 2 + c
    twin = z * 2 + 1 - c
    gathers = [{} for _ in range(CHUNKS)]

    def send(n, number, block, side, target):
        place = tokens.at[n, block]
        if side is not None:
            place = place.at[pl.ds(side * 2 * PAIRS, 2 * PAIRS)]
        copy = pltpu.make_async_remote_copy(
            src_ref=place, dst_ref=place,
            send_sem=ag_s.at[n, number], recv_sem=ag_r.at[n, number],
            device_id=(g, target), device_id_type=MESH,
        )
        copy.start()
        gathers[n][number] = copy

    squares = [jnp.zeros((2 * PAIRS, 1), F32)]

    def own(n):
        for copy in row_copies[n]:
            copy.wait_recv()
        got = dot(pack, arrived[n].reshape(SLOTS, piece))
        for h in range(2):
            one = got[h * 2 * PAIRS : (h + 1) * 2 * PAIRS]
            cols = pl.ds(h * half + n * piece, piece)
            squares[0] = squares[0] + jnp.sum(one * one, axis=1, keepdims=True)
            tokens[n, t, pl.ds(h * 2 * PAIRS, 2 * PAIRS), :] = (one * gain_ref[:, cols]).astype(
                BF16
            )
            resid[:, cols] = (one[:PAIRS] + one[PAIRS:]) * (1.0 / 16.0)
        for number, target in ((0, up), (1, down), (2, twin)):
            send(n, number, t, None, target)

    def forward_near(n):
        gathers[n][0].wait_recv()
        send(n, 3, down, 0, up)
        send(n, 4, down, None, twin)
        gathers[n][1].wait_recv()
        send(n, 5, up, 1, down)
        send(n, 6, up, None, twin)

    def forward_far(n):
        gathers[n][3].wait_recv()
        gathers[n][5].wait_recv()
        send(n, 7, far, None, twin)

    depth = 512

    def project(n):
        for number in (2, 4, 6, 7):
            gathers[n][number].wait_recv()

        def block(h, i):
            cols = pl.ds(pl.multiple_of(i * depth, depth), depth)
            a = tokens[n, :, pl.ds(h * 2 * PAIRS, 2 * PAIRS), cols]
            w = qkv_w[pl.ds(pl.multiple_of(h * half + n * piece + i * depth, depth), depth), :]
            return dot(a.reshape(2 * TENSORS * PAIRS, depth), w)

        if n == 0:
            acc[...] = jnp.zeros_like(acc)
        for h in range(2):

            @pl.loop(0, piece // depth)
            def _(i):
                acc[...] += block(h, i)

    factors = []
    for step in range(CHUNKS + 2):
        if step < CHUNKS:
            own(step)
        if step == CHUNKS - 1:
            factor = lax.rsqrt(squares[0] / width + 1e-05)
            scales[t] = jnp.broadcast_to(factor, (2 * PAIRS, 128))
            for j in range(1, TENSORS):
                copy = pltpu.make_async_remote_copy(
                    src_ref=scales.at[t], dst_ref=scales.at[t],
                    send_sem=sc_s.at[j], recv_sem=sc_r.at[j],
                    device_id=(g, ((z + j // 2) % SIDE) * 2 + (c + j % 2) % 2),
                    device_id_type=MESH,
                )
                copy.start()
                factors.append(copy)
        if 0 <= step - 1 < CHUNKS:
            forward_near(step - 1)
        if step - 2 >= 0:
            if step == 2:
                for copy in loads[4:7]:
                    copy.wait()
            forward_far(step - 2)
            project(step - 2)
    for copy in factors:
        copy.wait_recv()

    count = 2 * TENSORS * PAIRS
    factor = scales[...].reshape(count, 128)

    def column(at):
        return acc[:, pl.ds(at * HEAD_DIM, HEAD_DIM)] * factor

    def unit(rows_):
        return (
            rows_ * lax.rsqrt(jnp.mean(rows_ * rows_, axis=-1, keepdims=True) + 1e-06)
        ).astype(BF16)

    heads = q_cols // HEAD_DIM
    key = unit(column(heads))
    value = column(heads + 1).astype(BF16)
    mask = (iota((count, count), 0) % PAIRS) == (iota((count, count), 1) % PAIRS)
    pool = jnp.where(
        iota((PAIRS, count), 0) == iota((PAIRS, count), 1) % PAIRS, 1.0, 0.0
    ).astype(BF16)
    pooled = []
    for head in range(heads):
        query = unit(column(head))
        scores = lax.dot_general(
            query, key, (((1,), (1,)), ((), ())), preferred_element_type=F32
        ) * (SCORE_SCALE / HEAD_DIM)
        expo = jnp.where(mask, jnp.exp(scores), 0.0)
        weights = (expo * (1.0 / jnp.sum(expo, axis=-1, keepdims=True))).astype(BF16)
        context = dot(weights, value).astype(BF16)
        pooled.append(dot(pool, context) * (1.0 / 16.0))
    pooled = jnp.concatenate(pooled, axis=1)
    high = pooled.astype(BF16)
    low = (pooled - high.astype(F32)).astype(BF16)
    both = jnp.concatenate([high, low], axis=0)

    loads[7].wait()
    sums = []
    for j in (4, 5, 2, 3, 6, 7, 1, 0):
        target = ((z + j // 2) % SIDE) * 2 + (c + j % 2) % 2
        cols = pl.ds(pl.multiple_of(target * share, share), share)
        got = dot(both, out_w[:, cols])
        part[j] = got[:PAIRS] + got[PAIRS:] + resid[:, cols]
        if j > 0:
            copy = pltpu.make_async_remote_copy(
                src_ref=part.at[j], dst_ref=parts_in.at[j],
                send_sem=rs_s.at[j], recv_sem=rs_r.at[j],
                device_id=(g, target), device_id_type=MESH,
            )
            copy.start()
            sums.append(copy)
    for copy in sums:
        copy.wait_recv()
    total = part[0]
    for j in range(1, TENSORS):
        total = total + parts_in[j]
    live = iota((PAIRS, share), 0) < count_ref[...]
    total = jnp.where(live, total, 0.0)

    stacked = jnp.concatenate([total[:, : share // 2], total[:, share // 2 :]], axis=0)
    parts3 = pieces(stacked)
    got = dot(spread, parts3[0]) + dot(spread, parts3[1]) + dot(spread, parts3[2])
    fin_out[...] = got.reshape(GROUPS, 8, share // 2)
    finals = []
    for k in range(1, GROUPS):
        copy = pltpu.make_async_remote_copy(
            src_ref=fin_out.at[k], dst_ref=fin_in.at[k],
            send_sem=fin_s.at[k], recv_sem=fin_r.at[k],
            device_id=(group_shift(g, k, -1), t), device_id_type=MESH,
        )
        copy.start()
        finals.append(copy)
    fin_in[0] = fin_out[0]
    for copy in finals:
        copy.wait_recv()

    for copies in [idx, factors, sums, finals] + row_copies:
        for copy in copies:
            copy.wait_send()
    for copies in gathers:
        for copy in copies.values():
            copy.wait_send()


def owner_sums(wanted_ref, came_ref, lout_ref, rout_ref):
    pick = pick_matrix(wanted_ref[...].reshape(SLOTS, 128))
    span = came_ref.shape[2]
    got = jnp.zeros((4 * ROWS, span), F32)
    for one in pieces(came_ref[...].reshape(SLOTS, span)):
        got = got + lax.dot_general(
            pick, one, (((0,), (0,)), ((), ())), preferred_element_type=F32
        )
    for h in range(2):
        for side, out in enumerate((lout_ref, rout_ref)):
            at = (h * 2 + side) * ROWS
            out[:, pl.ds(h * span, span)] = got[at : at + ROWS]


def on_device(
    left_table, right_table, left_owner, left_row, right_owner, right_row, pair_count,
    norm_gain, query_weight, key_weight, value_weight, output_weight,
):
    width = left_table.shape[2]
    half = width // 2
    share = width // TENSORS
    piece = half // CHUNKS
    qkv = query_weight.shape[1] + 2 * key_weight.shape[1]
    vmem = pl.BlockSpec(memory_space=pltpu.VMEM)
    hbm = pl.BlockSpec(memory_space=pl.ANY)
    dma = pltpu.SemaphoreType.DMA
    wanted, came = pl.pallas_call(
        kernel,
        out_shape=(
            jax.ShapeDtypeStruct((GROUPS, 8, 128), F32),
            jax.ShapeDtypeStruct((GROUPS, 8, share // 2), F32),
        ),
        in_specs=[vmem] * 6 + [hbm] * 6,
        out_specs=(vmem, vmem),
        scratch_shapes=[
            pltpu.VMEM((4 * ROWS, half), BF16),
            pltpu.VMEM((width, qkv), BF16),
            pltpu.VMEM(output_weight.shape, BF16),
            pltpu.VMEM((GROUPS, 8, 128), F32),
            pltpu.VMEM((CHUNKS, GROUPS, 8, piece), BF16),
            pltpu.VMEM((CHUNKS, GROUPS, 8, piece), BF16),
            pltpu.VMEM((CHUNKS, TENSORS, 4 * PAIRS, piece), BF16),
            pltpu.VMEM((TENSORS, 2 * PAIRS, 128), F32),
            pltpu.VMEM((PAIRS, width), F32),
            pltpu.VMEM((2 * TENSORS * PAIRS, qkv), F32),
            pltpu.VMEM((TENSORS, PAIRS, share), F32),
            pltpu.VMEM((TENSORS, PAIRS, share), F32),
            pltpu.VMEM((GROUPS, 8, share // 2), F32),
            dma((8,)),
            dma((GROUPS,)), dma((GROUPS,)),
            dma((CHUNKS, GROUPS)), dma((CHUNKS, GROUPS)),
            dma((CHUNKS, 8)), dma((CHUNKS, 8)),
            dma((TENSORS,)), dma((TENSORS,)),
            dma((TENSORS,)), dma((TENSORS,)),
            dma((GROUPS,)), dma((GROUPS,)),
        ],
        compiler_params=pltpu.CompilerParams(
            collective_id=0, has_side_effects=True, vmem_limit_bytes=56 * 1024 * 1024
        ),
    )(
        left_owner.reshape(1, PAIRS), left_row.reshape(1, PAIRS),
        right_owner.reshape(1, PAIRS), right_row.reshape(1, PAIRS),
        pair_count.reshape(1, 1), norm_gain.reshape(1, width),
        left_table.reshape(ROWS, width), right_table.reshape(ROWS, width),
        query_weight, key_weight, value_weight, output_weight,
    )
    out = jax.ShapeDtypeStruct((ROWS, share), F32)
    return pl.pallas_call(
        owner_sums, out_shape=(out, out), in_specs=[vmem, vmem], out_specs=(vmem, vmem)
    )(wanted, came)


def solution(mesh):
    return jax.shard_map(
        on_device,
        mesh=mesh,
        in_specs=(
            P("group", "tensor", None), P("group", "tensor", None),
            P("group", None), P("group"), P("group", None), P("group"), P("group"), P(),
            P(None, "tensor"), P(None, "tensor"), P(None, "tensor"), P("tensor", None),
        ),
        out_specs=(P("group", "tensor"), P("group", "tensor")),
        check_vma=False,
    )
```

time: 74.6 us -> 70.1 us (0.940)
  local copies, waits for them, and re-layouts: 3.34 us -> 0 us
  Pallas kernels: 69.5 us -> 68.3 us
    unnamed x2 -> x0, local copies, waits for them, and re-layouts: 3.34 us -> none
    pallas_call x1 -> x2, Pallas kernels: 69.5 us -> 68.3 us  [the longest x1 66.1 us: on_device(): pl.pallas_call(kernel, out_shape=(jax.ShapeDtypeStruct((GROUPS, 8, 128),...]
where the time goes in v2:
time: 70.1 us; the launch traced here: 69.6 us
  Pallas kernels  68.3 us (97%)
  between operations  1.29 us (2%)
    pallas_call x1, Pallas kernels, on_device(): pl.pallas_call(kernel, out_shape=(jax.ShapeDtypeStruct((GROUPS, 8, 128),...  66.1 us
    pallas_call x1, Pallas kernels, on_device(): pl.pallas_call(owner_sums, out_shape=(out, out), in_specs=[vmem, vmem], o...  2.2 us

profile of v2, /device:TPU:0, one launch (start us, length us, event | category | flops | bytes accessed | tf_op | source)
XLA Modules:
  0.0 69.6 jit_solution(13325501738383208729)
XLA Ops:
  1.3 66.1 %shard_map.131 = (f32[16,8,128]{2,1,0:T(8,128)}, f32[16,8,512]{2,1,0:T(8,128)}) custom-call(s32[1,16]{1,0:T(1,128)} %bitcast.12, s32[1,16]{1,0:T(1,128)} %bitcast.13, s32[1,16]{1,0:T(1,128)} %bitcast.14, s32[1,16]{1,0:T(1,128)} %bitcast.15, s32[1,1]{1,0:T(1,128)} %bitcast.8.count_ref, f32[1,8192]{1,0:T(1,128)} %bitcast.11, bf16[64,8192]{1,0:T(8,128)(2,1)} %bitcast.9, ...), custom_call_target="tpu_custom_call" | custom-call | tf_op jit(solution)/shard_map/pallas_call | solution.py:400
  67.4 2.2 %shard_map.132 = (f32[64,1024]{1,0:T(8,128)}, f32[64,1024]{1,0:T(8,128)}) custom-call(f32[16,8,128]{2,1,0:T(8,128)} %get-tuple-element.4.wanted_ref, f32[16,8,512]{2,1,0:T(8,128)} %get-tuple-element.5.came_ref), custom_call_target="tpu_custom_call" | custom-call | tf_op jit(solution)/shard_map/pallas_call | solution.py:441

commit v3 on v2

--- a/solution.py
+++ b/solution.py
@@ -15,6 +15,14 @@
 SLOTS = GROUPS * 8
 ROWS = 64
 CHUNKS = 4
+AHEAD = 4
+LAG_NEAR = 1
+LAG_FAR = 2
+LAG_PROJECT = 3
+ORDER = sorted(
+    range(1, GROUPS),
+    key=lambda k: -(min(k // SIDE, SIDE - k // SIDE) + min(k % SIDE, SIDE - k % SIDE)),
+)
 F32 = jnp.float32
 BF16 = jnp.bfloat16
 
@@ -108,12 +116,14 @@
 
 
 def kernel(
-    lo_ref, lr_ref, ro_ref, rr_ref, count_ref, gain_ref,
+    lo_hbm, lr_hbm, ro_hbm, rr_hbm, count_hbm, gain_hbm,
     lt_ref, rt_ref, wq_ref, wk_ref, wv_ref, wo_ref,
-    inbox, fin_in,
+    wanted, fin_in,
+    lo_ref, lr_ref, ro_ref, rr_ref, count_ref, gain_ref, inbox,
     table, qkv_w, out_w, outbox, picked, arrived, tokens, scales, resid,
-    acc, part, parts_in, fin_out,
-    load_sem, idx_s, idx_r, row_s, row_r, ag_s, ag_r, sc_s, sc_r, rs_s, rs_r, fin_s, fin_r,
+    acc, across, across_in, part, parts_in, fin_out,
+    load_sem, idx_s, idx_r, row_s, row_r, ag_s, ag_r, sc_s, sc_r, tw_s, tw_r, rs_s, rs_r,
+    fin_s, fin_r,
 ):
     g = lax.axis_index("group")
     t = lax.axis_index("tensor")
@@ -130,6 +140,10 @@
         copy.start()
         loads.append(copy)
 
+    for src, dst in (
+        (lo_hbm, lo_ref), (lr_hbm, lr_ref), (ro_hbm, ro_ref), (rr_hbm, rr_ref)
+    ):
+        load(src, dst)
     for h in range(2):
         for side, ref in enumerate((lt_ref, rt_ref)):
             load(
@@ -138,7 +152,7 @@
             )
 
     barrier = pltpu.get_barrier_semaphore()
-    for k in range(1, GROUPS):
+    for k in ORDER:
         pl.semaphore_signal(
             barrier, inc=1, device_id=(group_shift(g, k, 1), t), device_id_type=MESH
         )
@@ -149,11 +163,15 @@
 
     q_cols = wq_ref.shape[1]
     kv_cols = wk_ref.shape[1]
+    load(gain_hbm, gain_ref)
+    load(count_hbm, count_ref)
     load(wq_ref, qkv_w.at[:, pl.ds(0, q_cols)])
     load(wk_ref, qkv_w.at[:, pl.ds(q_cols, kv_cols)])
     load(wv_ref, qkv_w.at[:, pl.ds(q_cols + kv_cols, kv_cols)])
     load(wo_ref, out_w)
 
+    for copy in loads[:4]:
+        copy.wait()
     rows = (lr_ref[...].astype(F32), rr_ref[...].astype(F32))
     keys = [slot_keys(ref[...].astype(F32), g) for ref in (lo_ref, ro_ref)]
     asked = requests([key[0] for key in keys], rows, g)
@@ -164,7 +182,7 @@
     pl.semaphore_wait(barrier, GROUPS - 1 + TENSORS - 1)
 
     idx = []
-    for k in range(1, GROUPS):
+    for k in ORDER:
         copy = pltpu.make_async_remote_copy(
             src_ref=outbox.at[k], dst_ref=inbox.at[k],
             send_sem=idx_s.at[k], recv_sem=idx_r.at[k],
@@ -173,27 +191,31 @@
         copy.start()
         idx.append(copy)
     inbox[0] = outbox[0]
-    for copy in loads[:4]:
+    for copy in loads[4:10]:
         copy.wait()
     for copy in idx:
         copy.wait_recv()
+    load(inbox, wanted)
 
     pick = pick_matrix(inbox[...].reshape(SLOTS, 128))
-    row_copies = []
-    for n in range(CHUNKS):
-        rows_n = dot(pick, table[:, pl.ds(n * piece, piece)])
-        picked[n] = rows_n.astype(BF16).reshape(GROUPS, 8, piece)
-        copies = []
-        for k in range(1, GROUPS):
+    def ask(n):
+        for k in ORDER:
             copy = pltpu.make_async_remote_copy(
                 src_ref=picked.at[n, k], dst_ref=arrived.at[n, k],
                 send_sem=row_s.at[n, k], recv_sem=row_r.at[n, k],
                 device_id=(group_shift(g, k, 1), t), device_id_type=MESH,
             )
             copy.start()
-            copies.append(copy)
+            copies[n].append(copy)
+
+    copies = [[] for _ in range(CHUNKS)]
+    for n in range(CHUNKS):
+        rows_n = dot(pick, table[:, pl.ds(n * piece, piece)])
+        picked[n] = rows_n.astype(BF16).reshape(GROUPS, 8, piece)
+        if n < AHEAD:
+            ask(n)
         arrived[n, 0] = picked[n, 0]
-        row_copies.append(copies)
+    row_copies = copies
 
     up = ((z + 1) % SIDE) * 2 + c
     down = ((z + SIDE - 1) % SIDE) * 2 + c
@@ -218,6 +240,8 @@
     def own(n):
         for copy in row_copies[n]:
             copy.wait_recv()
+        if n + AHEAD < CHUNKS:
+            ask(n + AHEAD)
         got = dot(pack, arrived[n].reshape(SLOTS, piece))
         for h in range(2):
             one = got[h * 2 * PAIRS : (h + 1) * 2 * PAIRS]
@@ -264,7 +288,7 @@
                 acc[...] += block(h, i)
 
     factors = []
-    for step in range(CHUNKS + 2):
+    for step in range(CHUNKS + LAG_PROJECT):
         if step < CHUNKS:
             own(step)
         if step == CHUNKS - 1:
@@ -279,14 +303,15 @@
                 )
                 copy.start()
                 factors.append(copy)
-        if 0 <= step - 1 < CHUNKS:
-            forward_near(step - 1)
-        if step - 2 >= 0:
-            if step == 2:
-                for copy in loads[4:7]:
+        if 0 <= step - LAG_NEAR < CHUNKS:
+            forward_near(step - LAG_NEAR)
+        if 0 <= step - LAG_FAR < CHUNKS:
+            forward_far(step - LAG_FAR)
+        if step >= LAG_PROJECT:
+            if step == LAG_PROJECT:
+                for copy in loads[10:13]:
                     copy.wait()
-            forward_far(step - 2)
-            project(step - 2)
+            project(step - LAG_PROJECT)
     for copy in factors:
         copy.wait_recv()
 
@@ -323,26 +348,38 @@
     low = (pooled - high.astype(F32)).astype(BF16)
     both = jnp.concatenate([high, low], axis=0)
 
-    loads[7].wait()
+    loads[13].wait()
     sums = []
-    for j in (4, 5, 2, 3, 6, 7, 1, 0):
-        target = ((z + j // 2) % SIDE) * 2 + (c + j % 2) % 2
-        cols = pl.ds(pl.multiple_of(target * share, share), share)
+
+    def partial(dz, core):
+        cols = pl.ds(pl.multiple_of((((z + dz) % SIDE) * 2 + core) * share, share), share)
         got = dot(both, out_w[:, cols])
-        part[j] = got[:PAIRS] + got[PAIRS:] + resid[:, cols]
-        if j > 0:
-            copy = pltpu.make_async_remote_copy(
-                src_ref=part.at[j], dst_ref=parts_in.at[j],
-                send_sem=rs_s.at[j], recv_sem=rs_r.at[j],
-                device_id=(g, target), device_id_type=MESH,
-            )
-            copy.start()
-            sums.append(copy)
-    for copy in sums:
+        return got[:PAIRS] + got[PAIRS:] + resid[:, cols]
+
+    def push(source, target_ref, sends, recvs, at, target):
+        copy = pltpu.make_async_remote_copy(
+            src_ref=source.at[at], dst_ref=target_ref.at[at],
+            send_sem=sends.at[at], recv_sem=recvs.at[at],
+            device_id=(g, target), device_id_type=MESH,
+        )
+        copy.start()
+        sums.append(copy)
+        return copy
+
+    crossing = {}
+    for dz in (2, 1, 3, 0):
+        across[dz] = partial(dz, 1 - c)
+        crossing[dz] = push(across, across_in, tw_s, tw_r, dz, twin)
+    coming = []
+    for dz in (2, 1, 3, 0):
+        mine = partial(dz, c)
+        crossing[dz].wait_recv()
+        part[dz] = mine + across_in[dz]
+        if dz > 0:
+            coming.append(push(part, parts_in, rs_s, rs_r, dz, ((z + dz) % SIDE) * 2 + c))
+    for copy in coming:
         copy.wait_recv()
-    total = part[0]
-    for j in range(1, TENSORS):
-        total = total + parts_in[j]
+    total = part[0] + parts_in[1] + parts_in[2] + parts_in[3]
     live = iota((PAIRS, share), 0) < count_ref[...]
     total = jnp.where(live, total, 0.0)
 
@@ -351,7 +388,7 @@
     got = dot(spread, parts3[0]) + dot(spread, parts3[1]) + dot(spread, parts3[2])
     fin_out[...] = got.reshape(GROUPS, 8, share // 2)
     finals = []
-    for k in range(1, GROUPS):
+    for k in ORDER:
         copy = pltpu.make_async_remote_copy(
             src_ref=fin_out.at[k], dst_ref=fin_in.at[k],
             send_sem=fin_s.at[k], recv_sem=fin_r.at[k],
@@ -359,10 +396,12 @@
         )
         copy.start()
         finals.append(copy)
-    fin_in[0] = fin_out[0]
+    load(fin_out.at[0], fin_in.at[0])
     for copy in finals:
         copy.wait_recv()
 
+    for copy in loads[14:]:
+        copy.wait()
     for copies in [idx, factors, sums, finals] + row_copies:
         for copy in copies:
             copy.wait_send()
@@ -403,9 +442,16 @@
             jax.ShapeDtypeStruct((GROUPS, 8, 128), F32),
             jax.ShapeDtypeStruct((GROUPS, 8, share // 2), F32),
         ),
-        in_specs=[vmem] * 6 + [hbm] * 6,
-        out_specs=(vmem, vmem),
+        in_specs=[hbm] * 12,
+        out_specs=(hbm, hbm),
         scratch_shapes=[
+            pltpu.VMEM((1, PAIRS), jnp.int32),
+            pltpu.VMEM((1, PAIRS), jnp.int32),
+            pltpu.VMEM((1, PAIRS), jnp.int32),
+            pltpu.VMEM((1, PAIRS), jnp.int32),
+            pltpu.VMEM((1, 1), jnp.int32),
+            pltpu.VMEM((1, width), F32),
+            pltpu.VMEM((GROUPS, 8, 128), F32),
             pltpu.VMEM((4 * ROWS, half), BF16),
             pltpu.VMEM((width, qkv), BF16),
             pltpu.VMEM(output_weight.shape, BF16),
@@ -416,15 +462,18 @@
             pltpu.VMEM((TENSORS, 2 * PAIRS, 128), F32),
             pltpu.VMEM((PAIRS, width), F32),
             pltpu.VMEM((2 * TENSORS * PAIRS, qkv), F32),
-            pltpu.VMEM((TENSORS, PAIRS, share), F32),
-            pltpu.VMEM((TENSORS, PAIRS, share), F32),
+            pltpu.VMEM((SIDE, PAIRS, share), F32),
+            pltpu.VMEM((SIDE, PAIRS, share), F32),
+            pltpu.VMEM((SIDE, PAIRS, share), F32),
+            pltpu.VMEM((SIDE, PAIRS, share), F32),
             pltpu.VMEM((GROUPS, 8, share // 2), F32),
-            dma((8,)),
+            dma((16,)),
             dma((GROUPS,)), dma((GROUPS,)),
             dma((CHUNKS, GROUPS)), dma((CHUNKS, GROUPS)),
             dma((CHUNKS, 8)), dma((CHUNKS, 8)),
             dma((TENSORS,)), dma((TENSORS,)),
-            dma((TENSORS,)), dma((TENSORS,)),
+            dma((SIDE,)), dma((SIDE,)),
+            dma((SIDE,)), dma((SIDE,)),
             dma((GROUPS,)), dma((GROUPS,)),
         ],
         compiler_params=pltpu.CompilerParams(

time: 70.1 us -> 64 us (0.913)
  Pallas kernels: 68.3 us -> 61.7 us
    pallas_call x1, Pallas kernels: 66.1 us -> 59.5 us  [on_device(): pl.pallas_call(kernel, out_shape=(jax.ShapeDtypeStruct((GROUPS, 8, 128),...]
where the time goes in v3:
time: 64 us; the launch traced here: 62.9 us
  Pallas kernels  61.7 us (96%)
  between operations  1.29 us (2%)
    pallas_call x1, Pallas kernels, on_device(): pl.pallas_call(kernel, out_shape=(jax.ShapeDtypeStruct((GROUPS, 8, 128),...  59.5 us
    pallas_call x1, Pallas kernels, on_device(): pl.pallas_call(owner_sums, out_shape=(out, out), in_specs=[vmem, vmem], o...  2.2 us

profile of v3, /device:TPU:0, one launch (start us, length us, event | category | flops | bytes accessed | tf_op | source)
XLA Modules:
  0.0 62.9 jit_solution(3563260985038330055)
XLA Ops:
  1.3 59.5 %shard_map.131 = (f32[16,8,128]{2,1,0:T(8,128)}, f32[16,8,512]{2,1,0:T(8,128)}) custom-call(s32[1,16]{1,0:T(1,128)} %bitcast.12, s32[1,16]{1,0:T(1,128)} %bitcast.13, s32[1,16]{1,0:T(1,128)} %bitcast.14, s32[1,16]{1,0:T(1,128)} %bitcast.15, s32[1,1]{1,0:T(1,128)} %bitcast.8.count_hbm, f32[1,8192]{1,0:T(1,128)} %bitcast.11, bf16[64,8192]{1,0:T(8,128)(2,1)} %bitcast.9, ...), custom_call_target="tpu_custom_call" | custom-call | tf_op jit(solution)/shard_map/pallas_call | solution.py:439
  60.8 2.2 %shard_map.132 = (f32[64,1024]{1,0:T(8,128)}, f32[64,1024]{1,0:T(8,128)}) custom-call(f32[16,8,128]{2,1,0:T(8,128)} %get-tuple-element.4.wanted_ref, f32[16,8,512]{2,1,0:T(8,128)} %get-tuple-element.5.came_ref), custom_call_target="tpu_custom_call" | custom-call | tf_op jit(solution)/shard_map/pallas_call | solution.py:490

commit v4 on v3

--- a/solution.py
+++ b/solution.py
@@ -14,7 +14,10 @@
 PAIRS = 16
 SLOTS = GROUPS * 8
 ROWS = 64
-CHUNKS = 4
+PIECES = (1024, 1024, 1024, 1024)
+STARTS = tuple(sum(PIECES[:n]) for n in range(len(PIECES)))
+CHUNKS = len(PIECES)
+LEAD = 128
 AHEAD = 4
 LAG_NEAR = 1
 LAG_FAR = 2
@@ -62,8 +65,8 @@
     def place(owner, rank):
         whole = owner.astype(jnp.int32)
         y, x = me // SIDE, me % SIDE
-        ky = (y - whole // SIDE + SIDE) % SIDE
-        kx = (x - whole % SIDE + SIDE) % SIDE
+        ky = (y - (whole >> 2)) & 3
+        kx = (x - whole) & 3
         return ((ky * SIDE + kx) * 2).astype(F32) + rank
 
     return want_row, place(owner_row, rank_row), place(owner_col, rank_col)
@@ -71,13 +74,13 @@
 
 def slot_parts(shape, axis):
     at = iota(shape, axis)
-    return at // 8, (at % 8) // 4, (at % 4) // 2, at % 2
+    return at >> 3, (at >> 2) & 1, (at >> 1) & 1, at & 1
 
 
 def requests(want_rows, row_rows, me):
     k, _, side, rank = slot_parts((SLOTS, PAIRS), 0)
     y, x = me // SIDE, me % SIDE
-    owner = ((y - k // SIDE + SIDE) % SIDE) * SIDE + (x - k % SIDE + SIDE) % SIDE
+    owner = (((y - (k >> 2)) & 3) << 2) + ((x - k) & 3)
     want = (owner * 2 + rank).astype(F32)
     left = side == 0
     hit = jnp.where(left, want_rows[0], want_rows[1]) == want
@@ -90,7 +93,7 @@
     _, half, side, _ = slot_parts(shape, 0)
     lane = iota(shape, 1)
     both = jnp.concatenate([wanted, wanted], axis=1)
-    hit = (both == (lane % ROWS).astype(F32)) & (lane // ROWS == half * 2 + side)
+    hit = (both == (lane & 63).astype(F32)) & ((lane >> 6) == half * 2 + side)
     return jnp.where(hit, 1.0, 0.0).astype(BF16)
 
 
@@ -98,7 +101,7 @@
     shape = (4 * PAIRS, SLOTS)
     tall = jnp.concatenate(list(place_cols) * 2, axis=0)
     k, half, side, rank = slot_parts(shape, 1)
-    hit = (tall == (k * 2 + rank).astype(F32)) & (iota(shape, 0) // PAIRS == half * 2 + side)
+    hit = (tall == (k * 2 + rank).astype(F32)) & ((iota(shape, 0) >> 4) == half * 2 + side)
     return jnp.where(hit, 1.0, 0.0).astype(BF16)
 
 
@@ -107,7 +110,7 @@
     k, half, side, rank = slot_parts(shape, 0)
     wide = [jnp.concatenate([row, row], axis=1) for row in place_rows]
     key = (k * 2 + rank).astype(F32)
-    hit = (jnp.where(side == 0, wide[0], wide[1]) == key) & (iota(shape, 1) // PAIRS == half)
+    hit = (jnp.where(side == 0, wide[0], wide[1]) == key) & ((iota(shape, 1) >> 4) == half)
     return jnp.where(hit, 1.0, 0.0).astype(BF16)
 
 
@@ -120,36 +123,17 @@
     lt_ref, rt_ref, wq_ref, wk_ref, wv_ref, wo_ref,
     wanted, fin_in,
     lo_ref, lr_ref, ro_ref, rr_ref, count_ref, gain_ref, inbox,
-    table, qkv_w, out_w, outbox, picked, arrived, tokens, scales, resid,
+    table, qkv_w, out_w, outbox, picked, arrived, resid,
     acc, across, across_in, part, parts_in, fin_out,
-    load_sem, idx_s, idx_r, row_s, row_r, ag_s, ag_r, sc_s, sc_r, tw_s, tw_r, rs_s, rs_r,
-    fin_s, fin_r,
+    load_sem, idx_s, idx_r, row_s, row_r, ag_s, ag_r, tw_s, tw_r, rs_s, rs_r,
+    fin_s, fin_r, *tokens,
 ):
     g = lax.axis_index("group")
     t = lax.axis_index("tensor")
     z, c = t // 2, t % 2
     width = out_w.shape[1]
     half = width // 2
-    piece = half // CHUNKS
     share = width // TENSORS
-
-    loads = []
-
-    def load(src, dst):
-        copy = pltpu.make_async_copy(src, dst, load_sem.at[len(loads)])
-        copy.start()
-        loads.append(copy)
-
-    for src, dst in (
-        (lo_hbm, lo_ref), (lr_hbm, lr_ref), (ro_hbm, ro_ref), (rr_hbm, rr_ref)
-    ):
-        load(src, dst)
-    for h in range(2):
-        for side, ref in enumerate((lt_ref, rt_ref)):
-            load(
-                ref.at[:, pl.ds(h * half, half)],
-                table.at[pl.ds((h * 2 + side) * ROWS, ROWS), :],
-            )
 
     barrier = pltpu.get_barrier_semaphore()
     for k in ORDER:
@@ -160,6 +144,24 @@
         pl.semaphore_signal(
             barrier, inc=1, device_id=(g, (t + j) % TENSORS), device_id_type=MESH
         )
+
+    loads = []
+
+    def load(src, dst):
+        copy = pltpu.make_async_copy(src, dst, load_sem.at[len(loads)])
+        copy.start()
+        loads.append(copy)
+
+    for src, dst in (
+        (lo_hbm, lo_ref), (lr_hbm, lr_ref), (ro_hbm, ro_ref), (rr_hbm, rr_ref)
+    ):
+        load(src, dst)
+    for h in range(2):
+        for side, ref in enumerate((lt_ref, rt_ref)):
+            load(
+                ref.at[:, pl.ds(h * half, half)],
+                table.at[pl.ds((h * 2 + side) * ROWS, ROWS), pl.ds(LEAD, half)],
+            )
 
     q_cols = wq_ref.shape[1]
     kv_cols = wk_ref.shape[1]
@@ -193,15 +195,38 @@
     inbox[0] = outbox[0]
     for copy in loads[4:10]:
         copy.wait()
+    block = half // 8
+
+    def squares(i, sums):
+        at = pl.ds(pl.multiple_of(LEAD + i * block, 128), block)
+        values = table[:, at].astype(F32)
+        values = values * values
+        for n in range(block // 128):
+            sums = sums + values[:, n * 128 : (n + 1) * 128]
+        return sums
+
+    sums = lax.fori_loop(0, 8, squares, jnp.zeros((4 * ROWS, 128), F32))
+    sums = jnp.sum(sums[: 2 * ROWS] + sums[2 * ROWS :], axis=1, keepdims=True)
+    lane = iota((2 * ROWS, LEAD), 1)
+    lead = jnp.zeros((2 * ROWS, LEAD), F32)
+    for n, one in enumerate(pieces(lax.rsqrt(sums / width + 1e-05))):
+        lead = jnp.where(lane == n, one.astype(F32), lead)
+    lead = lead.astype(BF16)
+    table[pl.ds(0, 2 * ROWS), pl.ds(0, LEAD)] = lead
+    table[pl.ds(2 * ROWS, 2 * ROWS), pl.ds(0, LEAD)] = lead
     for copy in idx:
         copy.wait_recv()
     load(inbox, wanted)
 
     pick = pick_matrix(inbox[...].reshape(SLOTS, 128))
+    def chunk(n):
+        return pl.ds(0, LEAD + PIECES[0]) if n == 0 else pl.ds(LEAD + STARTS[n], PIECES[n])
+
     def ask(n):
+        span = chunk(n)
         for k in ORDER:
             copy = pltpu.make_async_remote_copy(
-                src_ref=picked.at[n, k], dst_ref=arrived.at[n, k],
+                src_ref=picked.at[k, :, span], dst_ref=arrived.at[k, :, span],
                 send_sem=row_s.at[n, k], recv_sem=row_r.at[n, k],
                 device_id=(group_shift(g, k, 1), t), device_id_type=MESH,
             )
@@ -210,11 +235,12 @@
 
     copies = [[] for _ in range(CHUNKS)]
     for n in range(CHUNKS):
-        rows_n = dot(pick, table[:, pl.ds(n * piece, piece)])
-        picked[n] = rows_n.astype(BF16).reshape(GROUPS, 8, piece)
+        span = chunk(n)
+        rows_n = dot(pick, table[:, span])
+        picked[:, :, span] = rows_n.astype(BF16).reshape(GROUPS, 8, span.size)
         if n < AHEAD:
             ask(n)
-        arrived[n, 0] = picked[n, 0]
+        arrived[0, :, span] = picked[0, :, span]
     row_copies = copies
 
     up = ((z + 1) % SIDE) * 2 + c
@@ -224,7 +250,7 @@
     gathers = [{} for _ in range(CHUNKS)]
 
     def send(n, number, block, side, target):
-        place = tokens.at[n, block]
+        place = tokens[n].at[block]
         if side is not None:
             place = place.at[pl.ds(side * 2 * PAIRS, 2 * PAIRS)]
         copy = pltpu.make_async_remote_copy(
@@ -235,21 +261,25 @@
         copy.start()
         gathers[n][number] = copy
 
-    squares = [jnp.zeros((2 * PAIRS, 1), F32)]
+    factor = []
 
     def own(n):
         for copy in row_copies[n]:
             copy.wait_recv()
         if n + AHEAD < CHUNKS:
             ask(n + AHEAD)
-        got = dot(pack, arrived[n].reshape(SLOTS, piece))
+        piece = PIECES[n]
+        if n == 0:
+            led = dot(pack, arrived[:, :, pl.ds(0, LEAD)].reshape(SLOTS, LEAD))
+            led = led[: 2 * PAIRS]
+            factor.append(led[:, 0:1] + led[:, 1:2] + led[:, 2:3])
+        got = dot(pack, arrived[:, :, pl.ds(LEAD + STARTS[n], piece)].reshape(SLOTS, piece))
         for h in range(2):
             one = got[h * 2 * PAIRS : (h + 1) * 2 * PAIRS]
-            cols = pl.ds(h * half + n * piece, piece)
-            squares[0] = squares[0] + jnp.sum(one * one, axis=1, keepdims=True)
-            tokens[n, t, pl.ds(h * 2 * PAIRS, 2 * PAIRS), :] = (one * gain_ref[:, cols]).astype(
-                BF16
-            )
+            cols = pl.ds(h * half + STARTS[n], piece)
+            tokens[n][t, pl.ds(h * 2 * PAIRS, 2 * PAIRS), :] = (
+                one * factor[0] * gain_ref[:, cols]
+            ).astype(BF16)
             resid[:, cols] = (one[:PAIRS] + one[PAIRS:]) * (1.0 / 16.0)
         for number, target in ((0, up), (1, down), (2, twin)):
             send(n, number, t, None, target)
@@ -267,42 +297,29 @@
         gathers[n][5].wait_recv()
         send(n, 7, far, None, twin)
 
-    depth = 512
-
     def project(n):
         for number in (2, 4, 6, 7):
             gathers[n][number].wait_recv()
+        depth = 512 if PIECES[n] % 512 == 0 else 256
 
         def block(h, i):
             cols = pl.ds(pl.multiple_of(i * depth, depth), depth)
-            a = tokens[n, :, pl.ds(h * 2 * PAIRS, 2 * PAIRS), cols]
-            w = qkv_w[pl.ds(pl.multiple_of(h * half + n * piece + i * depth, depth), depth), :]
+            a = tokens[n][:, pl.ds(h * 2 * PAIRS, 2 * PAIRS), cols]
+            start = pl.multiple_of(h * half + STARTS[n] + i * depth, 256)
+            w = qkv_w[pl.ds(start, depth), :]
             return dot(a.reshape(2 * TENSORS * PAIRS, depth), w)
 
         if n == 0:
             acc[...] = jnp.zeros_like(acc)
         for h in range(2):
 
-            @pl.loop(0, piece // depth)
+            @pl.loop(0, PIECES[n] // depth)
             def _(i):
                 acc[...] += block(h, i)
 
-    factors = []
     for step in range(CHUNKS + LAG_PROJECT):
         if step < CHUNKS:
             own(step)
-        if step == CHUNKS - 1:
-            factor = lax.rsqrt(squares[0] / width + 1e-05)
-            scales[t] = jnp.broadcast_to(factor, (2 * PAIRS, 128))
-            for j in range(1, TENSORS):
-                copy = pltpu.make_async_remote_copy(
-                    src_ref=scales.at[t], dst_ref=scales.at[t],
-                    send_sem=sc_s.at[j], recv_sem=sc_r.at[j],
-                    device_id=(g, ((z + j // 2) % SIDE) * 2 + (c + j % 2) % 2),
-                    device_id_type=MESH,
-                )
-                copy.start()
-                factors.append(copy)
         if 0 <= step - LAG_NEAR < CHUNKS:
             forward_near(step - LAG_NEAR)
         if 0 <= step - LAG_FAR < CHUNKS:
@@ -312,14 +329,11 @@
                 for copy in loads[10:13]:
                     copy.wait()
             project(step - LAG_PROJECT)
-    for copy in factors:
-        copy.wait_recv()
 
     count = 2 * TENSORS * PAIRS
-    factor = scales[...].reshape(count, 128)
 
     def column(at):
-        return acc[:, pl.ds(at * HEAD_DIM, HEAD_DIM)] * factor
+        return acc[:, pl.ds(at * HEAD_DIM, HEAD_DIM)]
 
     def unit(rows_):
         return (
@@ -329,9 +343,9 @@
     heads = q_cols // HEAD_DIM
     key = unit(column(heads))
     value = column(heads + 1).astype(BF16)
-    mask = (iota((count, count), 0) % PAIRS) == (iota((count, count), 1) % PAIRS)
+    mask = (iota((count, count), 0) & 15) == (iota((count, count), 1) & 15)
     pool = jnp.where(
-        iota((PAIRS, count), 0) == iota((PAIRS, count), 1) % PAIRS, 1.0, 0.0
+        iota((PAIRS, count), 0) == (iota((PAIRS, count), 1) & 15), 1.0, 0.0
     ).astype(BF16)
     pooled = []
     for head in range(heads):
@@ -374,19 +388,21 @@
     for dz in (2, 1, 3, 0):
         mine = partial(dz, c)
         crossing[dz].wait_recv()
-        part[dz] = mine + across_in[dz]
+        mine = mine + across_in[dz]
         if dz > 0:
+            part[dz] = mine.astype(BF16)
             coming.append(push(part, parts_in, rs_s, rs_r, dz, ((z + dz) % SIDE) * 2 + c))
     for copy in coming:
         copy.wait_recv()
-    total = part[0] + parts_in[1] + parts_in[2] + parts_in[3]
+    total = mine
+    for dz in (1, 2, 3):
+        total = total + parts_in[dz].astype(F32)
     live = iota((PAIRS, share), 0) < count_ref[...]
     total = jnp.where(live, total, 0.0)
 
     stacked = jnp.concatenate([total[:, : share // 2], total[:, share // 2 :]], axis=0)
-    parts3 = pieces(stacked)
-    got = dot(spread, parts3[0]) + dot(spread, parts3[1]) + dot(spread, parts3[2])
-    fin_out[...] = got.reshape(GROUPS, 8, share // 2)
+    got = dot(spread, stacked.astype(BF16))
+    fin_out[...] = got.astype(BF16).reshape(GROUPS, 8, share // 2)
     finals = []
     for k in ORDER:
         copy = pltpu.make_async_remote_copy(
@@ -397,27 +413,25 @@
         copy.start()
         finals.append(copy)
     load(fin_out.at[0], fin_in.at[0])
-    for copy in finals:
-        copy.wait_recv()
-
-    for copy in loads[14:]:
-        copy.wait()
-    for copies in [idx, factors, sums, finals] + row_copies:
+    for copies in [idx, sums] + row_copies:
         for copy in copies:
             copy.wait_send()
     for copies in gathers:
         for copy in copies.values():
             copy.wait_send()
+    for copy in loads[14:]:
+        copy.wait()
+    for copy in finals:
+        copy.wait()
 
 
 def owner_sums(wanted_ref, came_ref, lout_ref, rout_ref):
     pick = pick_matrix(wanted_ref[...].reshape(SLOTS, 128))
     span = came_ref.shape[2]
-    got = jnp.zeros((4 * ROWS, span), F32)
-    for one in pieces(came_ref[...].reshape(SLOTS, span)):
-        got = got + lax.dot_general(
-            pick, one, (((0,), (0,)), ((), ())), preferred_element_type=F32
-        )
+    got = lax.dot_general(
+        pick, came_ref[...].reshape(SLOTS, span), (((0,), (0,)), ((), ())),
+        preferred_element_type=F32,
+    )
     for h in range(2):
         for side, out in enumerate((lout_ref, rout_ref)):
             at = (h * 2 + side) * ROWS
@@ -431,7 +445,6 @@
     width = left_table.shape[2]
     half = width // 2
     share = width // TENSORS
-    piece = half // CHUNKS
     qkv = query_weight.shape[1] + 2 * key_weight.shape[1]
     vmem = pl.BlockSpec(memory_space=pltpu.VMEM)
     hbm = pl.BlockSpec(memory_space=pl.ANY)
@@ -440,7 +453,7 @@
         kernel,
         out_shape=(
             jax.ShapeDtypeStruct((GROUPS, 8, 128), F32),
-            jax.ShapeDtypeStruct((GROUPS, 8, share // 2), F32),
+            jax.ShapeDtypeStruct((GROUPS, 8, share // 2), BF16),
         ),
         in_specs=[hbm] * 12,
         out_specs=(hbm, hbm),
@@ -452,30 +465,28 @@
             pltpu.VMEM((1, 1), jnp.int32),
             pltpu.VMEM((1, width), F32),
             pltpu.VMEM((GROUPS, 8, 128), F32),
-            pltpu.VMEM((4 * ROWS, half), BF16),
+            pltpu.VMEM((4 * ROWS, LEAD + half), BF16),
             pltpu.VMEM((width, qkv), BF16),
             pltpu.VMEM(output_weight.shape, BF16),
             pltpu.VMEM((GROUPS, 8, 128), F32),
-            pltpu.VMEM((CHUNKS, GROUPS, 8, piece), BF16),
-            pltpu.VMEM((CHUNKS, GROUPS, 8, piece), BF16),
-            pltpu.VMEM((CHUNKS, TENSORS, 4 * PAIRS, piece), BF16),
-            pltpu.VMEM((TENSORS, 2 * PAIRS, 128), F32),
+            pltpu.VMEM((GROUPS, 8, LEAD + half), BF16),
+            pltpu.VMEM((GROUPS, 8, LEAD + half), BF16),
             pltpu.VMEM((PAIRS, width), F32),
             pltpu.VMEM((2 * TENSORS * PAIRS, qkv), F32),
             pltpu.VMEM((SIDE, PAIRS, share), F32),
             pltpu.VMEM((SIDE, PAIRS, share), F32),
-            pltpu.VMEM((SIDE, PAIRS, share), F32),
-            pltpu.VMEM((SIDE, PAIRS, share), F32),
-            pltpu.VMEM((GROUPS, 8, share // 2), F32),
+            pltpu.VMEM((SIDE, PAIRS, share), BF16),
+            pltpu.VMEM((SIDE, PAIRS, share), BF16),
+            pltpu.VMEM((GROUPS, 8, share // 2), BF16),
             dma((16,)),
             dma((GROUPS,)), dma((GROUPS,)),
             dma((CHUNKS, GROUPS)), dma((CHUNKS, GROUPS)),
             dma((CHUNKS, 8)), dma((CHUNKS, 8)),
-            dma((TENSORS,)), dma((TENSORS,)),
             dma((SIDE,)), dma((SIDE,)),
             dma((SIDE,)), dma((SIDE,)),
             dma((GROUPS,)), dma((GROUPS,)),
-        ],
+        ]
+        + [pltpu.VMEM((TENSORS, 4 * PAIRS, piece), BF16) for piece in PIECES],
         compiler_params=pltpu.CompilerParams(
             collective_id=0, has_side_effects=True, vmem_limit_bytes=56 * 1024 * 1024
         ),

time: 64 us -> 60.4 us (0.944)
  Pallas kernels: 61.7 us -> 58.6 us
    pallas_call x1, Pallas kernels: 59.5 us -> 56.6 us  [on_device(): pl.pallas_call(kernel, out_shape=(jax.ShapeDtypeStruct((GROUPS, 8, 128),...]
where the time goes in v4:
time: 60.4 us; the launch traced here: 59.9 us
  Pallas kernels  58.6 us (97%)
  between operations  1.29 us (2%)
    pallas_call x1, Pallas kernels, on_device(): pl.pallas_call(kernel, out_shape=(jax.ShapeDtypeStruct((GROUPS, 8, 128),...  56.6 us
    pallas_call x1, Pallas kernels, on_device(): pl.pallas_call(owner_sums, out_shape=(out, out), in_specs=[vmem, vmem], o...  1.98 us

profile of v4, /device:TPU:0, one launch (start us, length us, event | category | flops | bytes accessed | tf_op | source)
XLA Modules:
  0.0 59.9 jit_solution(15032126741421971251)
XLA Ops:
  1.3 56.6 %shard_map.131 = (f32[16,8,128]{2,1,0:T(8,128)}, bf16[16,8,512]{2,1,0:T(8,128)(2,1)}) custom-call(s32[1,16]{1,0:T(1,128)} %bitcast.12, s32[1,16]{1,0:T(1,128)} %bitcast.13, s32[1,16]{1,0:T(1,128)} %bitcast.14, s32[1,16]{1,0:T(1,128)} %bitcast.15, s32[1,1]{1,0:T(1,128)} %bitcast.8.count_hbm, f32[1,8192]{1,0:T(1,128)} %bitcast.11, bf16[64,8192]{1,0:T(8,128)(2,1)} %bitcast.9, ...), custom_call_target="tpu_custom_call" | custom-call | tf_op jit(solution)/shard_map/pallas_call | solution.py:452
  57.9 2.0 %shard_map.132 = (f32[64,1024]{1,0:T(8,128)}, f32[64,1024]{1,0:T(8,128)}) custom-call(f32[16,8,128]{2,1,0:T(8,128)} %get-tuple-element.4.wanted_ref, bf16[16,8,512]{2,1,0:T(8,128)(2,1)} %get-tuple-element.5.came_ref), custom_call_target="tpu_custom_call" | custom-call | tf_op jit(solution)/shard_map/pallas_call | solution.py:501

commit v5 on v4

--- a/solution.py
+++ b/solution.py
@@ -114,6 +114,10 @@
     return jnp.where(hit, 1.0, 0.0).astype(BF16)
 
 
+def wait_bytes(ref, sem):
+    pltpu.make_async_copy(ref, ref, sem).wait()
+
+
 def dot(a, b):
     return jnp.dot(a, b, preferred_element_type=F32)
 
@@ -124,8 +128,8 @@
     wanted, fin_in,
     lo_ref, lr_ref, ro_ref, rr_ref, count_ref, gain_ref, inbox,
     table, qkv_w, out_w, outbox, picked, arrived, resid,
-    acc, across, across_in, part, parts_in, fin_out,
-    load_sem, idx_s, idx_r, row_s, row_r, ag_s, ag_r, tw_s, tw_r, rs_s, rs_r,
+    acc, part, parts_in, fin_out,
+    load_sem, idx_s, idx_r, row_s, row_r, ag_s, ag_r, rs_s, rs_r,
     fin_s, fin_r, *tokens,
 ):
     g = lax.axis_index("group")
@@ -183,15 +187,14 @@
 
     pl.semaphore_wait(barrier, GROUPS - 1 + TENSORS - 1)
 
-    idx = []
+    rest = pl.ds(1, GROUPS - 1)
     for k in ORDER:
         copy = pltpu.make_async_remote_copy(
             src_ref=outbox.at[k], dst_ref=inbox.at[k],
-            send_sem=idx_s.at[k], recv_sem=idx_r.at[k],
+            send_sem=idx_s, recv_sem=idx_r,
             device_id=(group_shift(g, k, -1), t), device_id_type=MESH,
         )
         copy.start()
-        idx.append(copy)
     inbox[0] = outbox[0]
     for copy in loads[4:10]:
         copy.wait()
@@ -214,8 +217,7 @@
     lead = lead.astype(BF16)
     table[pl.ds(0, 2 * ROWS), pl.ds(0, LEAD)] = lead
     table[pl.ds(2 * ROWS, 2 * ROWS), pl.ds(0, LEAD)] = lead
-    for copy in idx:
-        copy.wait_recv()
+    wait_bytes(inbox.at[rest], idx_r)
     load(inbox, wanted)
 
     pick = pick_matrix(inbox[...].reshape(SLOTS, 128))
@@ -227,13 +229,11 @@
         for k in ORDER:
             copy = pltpu.make_async_remote_copy(
                 src_ref=picked.at[k, :, span], dst_ref=arrived.at[k, :, span],
-                send_sem=row_s.at[n, k], recv_sem=row_r.at[n, k],
+                send_sem=row_s, recv_sem=row_r.at[n],
                 device_id=(group_shift(g, k, 1), t), device_id_type=MESH,
             )
             copy.start()
-            copies[n].append(copy)
-
-    copies = [[] for _ in range(CHUNKS)]
+
     for n in range(CHUNKS):
         span = chunk(n)
         rows_n = dot(pick, table[:, span])
@@ -241,31 +241,26 @@
         if n < AHEAD:
             ask(n)
         arrived[0, :, span] = picked[0, :, span]
-    row_copies = copies
 
     up = ((z + 1) % SIDE) * 2 + c
     down = ((z + SIDE - 1) % SIDE) * 2 + c
     far = ((z + 2) % SIDE) * 2 + c
     twin = z * 2 + 1 - c
-    gathers = [{} for _ in range(CHUNKS)]
-
     def send(n, number, block, side, target):
         place = tokens[n].at[block]
         if side is not None:
             place = place.at[pl.ds(side * 2 * PAIRS, 2 * PAIRS)]
         copy = pltpu.make_async_remote_copy(
             src_ref=place, dst_ref=place,
-            send_sem=ag_s.at[n, number], recv_sem=ag_r.at[n, number],
+            send_sem=ag_s.at[n], recv_sem=ag_r.at[n, number],
             device_id=(g, target), device_id_type=MESH,
         )
         copy.start()
-        gathers[n][number] = copy
 
     factor = []
 
     def own(n):
-        for copy in row_copies[n]:
-            copy.wait_recv()
+        wait_bytes(arrived.at[rest, :, chunk(n)], row_r.at[n])
         if n + AHEAD < CHUNKS:
             ask(n + AHEAD)
         piece = PIECES[n]
@@ -281,25 +276,23 @@
                 one * factor[0] * gain_ref[:, cols]
             ).astype(BF16)
             resid[:, cols] = (one[:PAIRS] + one[PAIRS:]) * (1.0 / 16.0)
-        for number, target in ((0, up), (1, down), (2, twin)):
+        for number, target in ((0, up), (1, down), (3, twin)):
             send(n, number, t, None, target)
 
     def forward_near(n):
-        gathers[n][0].wait_recv()
-        send(n, 3, down, 0, up)
-        send(n, 4, down, None, twin)
-        gathers[n][1].wait_recv()
-        send(n, 5, up, 1, down)
-        send(n, 6, up, None, twin)
+        wait_bytes(tokens[n].at[down], ag_r.at[n, 0])
+        send(n, 2, down, 0, up)
+        send(n, 3, down, None, twin)
+        wait_bytes(tokens[n].at[up], ag_r.at[n, 1])
+        send(n, 2, up, 1, down)
+        send(n, 3, up, None, twin)
 
     def forward_far(n):
-        gathers[n][3].wait_recv()
-        gathers[n][5].wait_recv()
-        send(n, 7, far, None, twin)
+        wait_bytes(tokens[n].at[far], ag_r.at[n, 2])
+        send(n, 3, far, None, twin)
 
     def project(n):
-        for number in (2, 4, 6, 7):
-            gathers[n][number].wait_recv()
+        wait_bytes(tokens[n].at[pl.ds(0, SIDE)], ag_r.at[n, 3])
         depth = 512 if PIECES[n] % 512 == 0 else 256
 
         def block(h, i):
@@ -336,93 +329,82 @@
         return acc[:, pl.ds(at * HEAD_DIM, HEAD_DIM)]
 
     def unit(rows_):
-        return (
-            rows_ * lax.rsqrt(jnp.mean(rows_ * rows_, axis=-1, keepdims=True) + 1e-06)
-        ).astype(BF16)
+        return rows_ * lax.rsqrt(jnp.mean(rows_ * rows_, axis=-1, keepdims=True) + 1e-06)
 
     heads = q_cols // HEAD_DIM
-    key = unit(column(heads))
-    value = column(heads + 1).astype(BF16)
-    mask = (iota((count, count), 0) & 15) == (iota((count, count), 1) & 15)
+    block = 8
+    rows_b = count // 2
+
+    def blocks(values):
+        tiles = values.reshape(rows_b // block, 2, block, HEAD_DIM)
+        return [tiles[:, n].reshape(rows_b, HEAD_DIM) for n in range(2)]
+
+    keys_b = blocks(unit(column(heads)))
+    values_b = blocks(column(heads + 1))
+    mask = (iota((rows_b, rows_b), 0) & 7) == (iota((rows_b, rows_b), 1) & 7)
     pool = jnp.where(
-        iota((PAIRS, count), 0) == (iota((PAIRS, count), 1) & 15), 1.0, 0.0
+        iota((block, rows_b), 0) == (iota((block, rows_b), 1) & 7), 1.0, 0.0
     ).astype(BF16)
     pooled = []
     for head in range(heads):
-        query = unit(column(head))
-        scores = lax.dot_general(
-            query, key, (((1,), (1,)), ((), ())), preferred_element_type=F32
-        ) * (SCORE_SCALE / HEAD_DIM)
-        expo = jnp.where(mask, jnp.exp(scores), 0.0)
-        weights = (expo * (1.0 / jnp.sum(expo, axis=-1, keepdims=True))).astype(BF16)
-        context = dot(weights, value).astype(BF16)
-        pooled.append(dot(pool, context) * (1.0 / 16.0))
+        halves = []
+        for n, query in enumerate(blocks(unit(column(head)))):
+            scores = lax.dot_general(
+                query.astype(BF16), keys_b[n].astype(BF16), (((1,), (1,)), ((), ())),
+                preferred_element_type=F32,
+            ) * (SCORE_SCALE / HEAD_DIM)
+            expo = jnp.where(mask, jnp.exp(scores), 0.0)
+            weights = (expo * (1.0 / jnp.sum(expo, axis=-1, keepdims=True))).astype(BF16)
+            context = dot(weights, values_b[n].astype(BF16)).astype(BF16)
+            halves.append(dot(pool, context) * (1.0 / 16.0))
+        pooled.append(jnp.concatenate(halves, axis=0))
     pooled = jnp.concatenate(pooled, axis=1)
     high = pooled.astype(BF16)
     low = (pooled - high.astype(F32)).astype(BF16)
     both = jnp.concatenate([high, low], axis=0)
 
     loads[13].wait()
-    sums = []
-
-    def partial(dz, core):
-        cols = pl.ds(pl.multiple_of((((z + dz) % SIDE) * 2 + core) * share, share), share)
+    for j in (4, 5, 2, 3, 6, 7, 1, 0):
+        target = ((z + j // 2) % SIDE) * 2 + (c + j % 2) % 2
+        cols = pl.ds(pl.multiple_of(target * share, share), share)
         got = dot(both, out_w[:, cols])
-        return got[:PAIRS] + got[PAIRS:] + resid[:, cols]
-
-    def push(source, target_ref, sends, recvs, at, target):
-        copy = pltpu.make_async_remote_copy(
-            src_ref=source.at[at], dst_ref=target_ref.at[at],
-            send_sem=sends.at[at], recv_sem=recvs.at[at],
-            device_id=(g, target), device_id_type=MESH,
-        )
-        copy.start()
-        sums.append(copy)
-        return copy
-
-    crossing = {}
-    for dz in (2, 1, 3, 0):
-        across[dz] = partial(dz, 1 - c)
-        crossing[dz] = push(across, across_in, tw_s, tw_r, dz, twin)
-    coming = []
-    for dz in (2, 1, 3, 0):
-        mine = partial(dz, c)
-        crossing[dz].wait_recv()
-        mine = mine + across_in[dz]
-        if dz > 0:
-            part[dz] = mine.astype(BF16)
-            coming.append(push(part, parts_in, rs_s, rs_r, dz, ((z + dz) % SIDE) * 2 + c))
-    for copy in coming:
-        copy.wait_recv()
+        mine = got[:PAIRS] + got[PAIRS:] + resid[:, cols]
+        if j > 0:
+            part[j] = mine.astype(BF16)
+            copy = pltpu.make_async_remote_copy(
+                src_ref=part.at[j], dst_ref=parts_in.at[j],
+                send_sem=rs_s, recv_sem=rs_r,
+                device_id=(g, target), device_id_type=MESH,
+            )
+            copy.start()
+    others = pl.ds(1, TENSORS - 1)
+    wait_bytes(parts_in.at[others], rs_r)
     total = mine
-    for dz in (1, 2, 3):
-        total = total + parts_in[dz].astype(F32)
+    for j in range(1, TENSORS):
+        total = total + parts_in[j].astype(F32)
     live = iota((PAIRS, share), 0) < count_ref[...]
     total = jnp.where(live, total, 0.0)
 
     stacked = jnp.concatenate([total[:, : share // 2], total[:, share // 2 :]], axis=0)
     got = dot(spread, stacked.astype(BF16))
     fin_out[...] = got.astype(BF16).reshape(GROUPS, 8, share // 2)
-    finals = []
     for k in ORDER:
         copy = pltpu.make_async_remote_copy(
             src_ref=fin_out.at[k], dst_ref=fin_in.at[k],
-            send_sem=fin_s.at[k], recv_sem=fin_r.at[k],
+            send_sem=fin_s, recv_sem=fin_r,
             device_id=(group_shift(g, k, -1), t), device_id_type=MESH,
         )
         copy.start()
-        finals.append(copy)
     load(fin_out.at[0], fin_in.at[0])
-    for copies in [idx, sums] + row_copies:
-        for copy in copies:
-            copy.wait_send()
-    for copies in gathers:
-        for copy in copies.values():
-            copy.wait_send()
+    wait_bytes(outbox.at[rest], idx_s)
+    wait_bytes(picked.at[rest], row_s)
+    for n in range(CHUNKS):
+        wait_bytes(tokens[n].at[pl.ds(0, TENSORS - 1)], ag_s.at[n])
+    wait_bytes(part.at[others], rs_s)
     for copy in loads[14:]:
         copy.wait()
-    for copy in finals:
-        copy.wait()
+    wait_bytes(fin_out.at[rest], fin_s)
+    wait_bytes(fin_in.at[rest], fin_r)
 
 
 def owner_sums(wanted_ref, came_ref, lout_ref, rout_ref):
@@ -473,18 +455,15 @@
             pltpu.VMEM((GROUPS, 8, LEAD + half), BF16),
             pltpu.VMEM((PAIRS, width), F32),
             pltpu.VMEM((2 * TENSORS * PAIRS, qkv), F32),
-            pltpu.VMEM((SIDE, PAIRS, share), F32),
-            pltpu.VMEM((SIDE, PAIRS, share), F32),
-            pltpu.VMEM((SIDE, PAIRS, share), BF16),
-            pltpu.VMEM((SIDE, PAIRS, share), BF16),
+            pltpu.VMEM((TENSORS, PAIRS, share), BF16),
+            pltpu.VMEM((TENSORS, PAIRS, share), BF16),
             pltpu.VMEM((GROUPS, 8, share // 2), BF16),
             dma((16,)),
-            dma((GROUPS,)), dma((GROUPS,)),
-            dma((CHUNKS, GROUPS)), dma((CHUNKS, GROUPS)),
-            dma((CHUNKS, 8)), dma((CHUNKS, 8)),
-            dma((SIDE,)), dma((SIDE,)),
-            dma((SIDE,)), dma((SIDE,)),
-            dma((GROUPS,)), dma((GROUPS,)),
+            dma, dma,
+            dma, dma((CHUNKS,)),
+            dma((CHUNKS,)), dma((CHUNKS, SIDE)),
+            dma, dma,
+            dma, dma,
         ]
         + [pltpu.VMEM((TENSORS, 4 * PAIRS, piece), BF16) for piece in PIECES],
         compiler_params=pltpu.CompilerParams(

time: 60.4 us -> 58 us (0.960)
  Pallas kernels: 58.6 us -> 56.1 us
    pallas_call x1, Pallas kernels: 56.6 us -> 54.1 us  [on_device(): pl.pallas_call(kernel, out_shape=(jax.ShapeDtypeStruct((GROUPS, 8, 128),...]
where the time goes in v5:
time: 58 us; the launch traced here: 57.4 us
  Pallas kernels  56.1 us (97%)
  between operations  1.29 us (2%)
    pallas_call x1, Pallas kernels, on_device(): pl.pallas_call(kernel, out_shape=(jax.ShapeDtypeStruct((GROUPS, 8, 128),...  54.1 us
    pallas_call x1, Pallas kernels, on_device(): pl.pallas_call(owner_sums, out_shape=(out, out), in_specs=[vmem, vmem], o...  1.98 us

profile of v5, /device:TPU:0, one launch (start us, length us, event | category | flops | bytes accessed | tf_op | source)
XLA Modules:
  0.0 57.4 jit_solution(5832198869374360204)
XLA Ops:
  1.3 54.1 %shard_map.131 = (f32[16,8,128]{2,1,0:T(8,128)}, bf16[16,8,512]{2,1,0:T(8,128)(2,1)}) custom-call(s32[1,16]{1,0:T(1,128)} %bitcast.12, s32[1,16]{1,0:T(1,128)} %bitcast.13, s32[1,16]{1,0:T(1,128)} %bitcast.14, s32[1,16]{1,0:T(1,128)} %bitcast.15, s32[1,1]{1,0:T(1,128)} %bitcast.8.count_hbm, f32[1,8192]{1,0:T(1,128)} %bitcast.11, bf16[64,8192]{1,0:T(8,128)(2,1)} %bitcast.9, ...), custom_call_target="tpu_custom_call" | custom-call | tf_op jit(solution)/shard_map/pallas_call | solution.py:434
  55.4 2.0 %shard_map.132 = (f32[64,1024]{1,0:T(8,128)}, f32[64,1024]{1,0:T(8,128)}) custom-call(f32[16,8,128]{2,1,0:T(8,128)} %get-tuple-element.4.wanted_ref, bf16[16,8,512]{2,1,0:T(8,128)(2,1)} %get-tuple-element.5.came_ref), custom_call_target="tpu_custom_call" | custom-call | tf_op jit(solution)/shard_map/pallas_call | solution.py:480

commit v6 on v5

--- a/solution.py
+++ b/solution.py
@@ -18,10 +18,7 @@
 STARTS = tuple(sum(PIECES[:n]) for n in range(len(PIECES)))
 CHUNKS = len(PIECES)
 LEAD = 128
-AHEAD = 4
-LAG_NEAR = 1
-LAG_FAR = 2
-LAG_PROJECT = 3
+AHEAD = 3
 ORDER = sorted(
     range(1, GROUPS),
     key=lambda k: -(min(k // SIDE, SIDE - k // SIDE) + min(k % SIDE, SIDE - k % SIDE)),
@@ -310,18 +307,17 @@
             def _(i):
                 acc[...] += block(h, i)
 
-    for step in range(CHUNKS + LAG_PROJECT):
-        if step < CHUNKS:
-            own(step)
-        if 0 <= step - LAG_NEAR < CHUNKS:
-            forward_near(step - LAG_NEAR)
-        if 0 <= step - LAG_FAR < CHUNKS:
-            forward_far(step - LAG_FAR)
-        if step >= LAG_PROJECT:
-            if step == LAG_PROJECT:
-                for copy in loads[10:13]:
-                    copy.wait()
-            project(step - LAG_PROJECT)
+    steps = (
+        (own, 0), (own, 1), (forward_near, 0), (own, 2),
+        (forward_near, 1), (own, 3), (forward_far, 0), (forward_near, 2),
+        (project, 0), (forward_far, 1), (forward_near, 3), (forward_far, 2),
+        (project, 1), (forward_far, 3), (project, 2), (project, 3),
+    )
+    for step, n in steps:
+        if step is project and n == 0:
+            for copy in loads[10:13]:
+                copy.wait()
+        step(n)
 
     count = 2 * TENSORS * PAIRS
 

time: 58 us -> 57.8 us (level)
  no operation moved by 1% of the time
where the time goes in v6:
time: 57.8 us; the launch traced here: 57.2 us
  Pallas kernels  55.9 us (97%)
  between operations  1.29 us (2%)
    pallas_call x1, Pallas kernels, on_device(): pl.pallas_call(kernel, out_shape=(jax.ShapeDtypeStruct((GROUPS, 8, 128),...  53.9 us
    pallas_call x1, Pallas kernels, on_device(): pl.pallas_call(owner_sums, out_shape=(out, out), in_specs=[vmem, vmem], o...  1.98 us

profile of v6, /device:TPU:0, one launch (start us, length us, event | category | flops | bytes accessed | tf_op | source)
XLA Modules:
  0.0 57.2 jit_solution(5545148744752062118)
XLA Ops:
  1.3 53.9 %shard_map.131 = (f32[16,8,128]{2,1,0:T(8,128)}, bf16[16,8,512]{2,1,0:T(8,128)(2,1)}) custom-call(s32[1,16]{1,0:T(1,128)} %bitcast.12, s32[1,16]{1,0:T(1,128)} %bitcast.13, s32[1,16]{1,0:T(1,128)} %bitcast.14, s32[1,16]{1,0:T(1,128)} %bitcast.15, s32[1,1]{1,0:T(1,128)} %bitcast.8.count_hbm, f32[1,8192]{1,0:T(1,128)} %bitcast.11, bf16[64,8192]{1,0:T(8,128)(2,1)} %bitcast.9, ...), custom_call_target="tpu_custom_call" | custom-call | tf_op jit(solution)/shard_map/pallas_call | solution.py:430
  55.2 2.0 %shard_map.132 = (f32[64,1024]{1,0:T(8,128)}, f32[64,1024]{1,0:T(8,128)}) custom-call(f32[16,8,128]{2,1,0:T(8,128)} %get-tuple-element.4.wanted_ref, bf16[16,8,512]{2,1,0:T(8,128)(2,1)} %get-tuple-element.5.came_ref), custom_call_target="tpu_custom_call" | custom-call | tf_op jit(solution)/shard_map/pallas_call | solution.py:476

commit v7 on v6

--- a/solution.py
+++ b/solution.py
@@ -300,10 +300,10 @@
             return dot(a.reshape(2 * TENSORS * PAIRS, depth), w)
 
         if n == 0:
-            acc[...] = jnp.zeros_like(acc)
+            acc[...] = block(0, 0)
         for h in range(2):
 
-            @pl.loop(0, PIECES[n] // depth)
+            @pl.loop(1 if n + h == 0 else 0, PIECES[n] // depth)
             def _(i):
                 acc[...] += block(h, i)
 

time: 57.8 us -> 57.9 us (level)
  no operation moved by 1% of the time
where the time goes in v7:
time: 57.9 us; the launch traced here: 57.1 us
  Pallas kernels  55.9 us (97%)
  between operations  1.29 us (2%)
    pallas_call x1, Pallas kernels, on_device(): pl.pallas_call(kernel, out_shape=(jax.ShapeDtypeStruct((GROUPS, 8, 128),...  53.9 us
    pallas_call x1, Pallas kernels, on_device(): pl.pallas_call(owner_sums, out_shape=(out, out), in_specs=[vmem, vmem], o...  1.98 us

profile of v7, /device:TPU:0, one launch (start us, length us, event | category | flops | bytes accessed | tf_op | source)
XLA Modules:
  0.0 57.1 jit_solution(4011419996340291370)
XLA Ops:
  1.3 53.9 %shard_map.131 = (f32[16,8,128]{2,1,0:T(8,128)}, bf16[16,8,512]{2,1,0:T(8,128)(2,1)}) custom-call(s32[1,16]{1,0:T(1,128)} %bitcast.12, s32[1,16]{1,0:T(1,128)} %bitcast.13, s32[1,16]{1,0:T(1,128)} %bitcast.14, s32[1,16]{1,0:T(1,128)} %bitcast.15, s32[1,1]{1,0:T(1,128)} %bitcast.8.count_hbm, f32[1,8192]{1,0:T(1,128)} %bitcast.11, bf16[64,8192]{1,0:T(8,128)(2,1)} %bitcast.9, ...), custom_call_target="tpu_custom_call" | custom-call | tf_op jit(solution)/shard_map/pallas_call | solution.py:430
  55.2 2.0 %shard_map.132 = (f32[64,1024]{1,0:T(8,128)}, f32[64,1024]{1,0:T(8,128)}) custom-call(f32[16,8,128]{2,1,0:T(8,128)} %get-tuple-element.4.wanted_ref, bf16[16,8,512]{2,1,0:T(8,128)(2,1)} %get-tuple-element.5.came_ref), custom_call_target="tpu_custom_call" | custom-call | tf_op jit(solution)/shard_map/pallas_call | solution.py:476
